TPU v7x, 32 devices: a whole 2x2x4 slice. The times are simulated.
32 devices in a mesh: gen: 4 (over x, core), bank: 8 (over z, y).
Axes of the slice: x: 2, y: 2, z: 4, core: 2. Of those that a mesh axis runs over, the one named last changes fastest.
Arguments:
- latents: bfloat16 [2048, 4096], P(('gen', 'bank')), may hold values from -6 to 6
- shift: bfloat16 [2048, 4096], P(('gen', 'bank')), may hold values from -3 to 3
- scale_mod: bfloat16 [2048, 4096], P(('gen', 'bank')), may hold values from -3 to 3
- head_weight: bfloat16 [4096, 1024], P('gen'), may hold values from -0.09375 to 0.09375
- bank: bfloat16 [16384, 1024], P('bank'), may hold values from -8 to 8
Outputs:
- update: float32 [4096, 1024], P(('gen', 'bank'))
All inputs are finite; a program needn't handle non-finite values.
Results may differ from a plain program's by a relative error of at most 0.0042.
Values may be sent and summed in bfloat16 or wider, within the bound.
No kernel may reach another device: no remote copies, remote signals or barrier semaphores. Data moves between devices by JAX's collectives and lax.ppermute only.
A program may use at most 128 MiB of HBM per device.

v0:
```python
import jax
import jax.numpy as jnp
from jax import lax
from jax.sharding import PartitionSpec as P

kernel_scale = 32.0


def local(latents, shift, scale_mod, head_weight, bank):
    samples = latents.shape[0]
    width = head_weight.shape[1]
    feats = latents.astype(jnp.float32)
    inverse = lax.rsqrt(jnp.mean(feats * feats, axis=1, keepdims=True) + 1e-06)
    hidden = (
        feats * inverse * (1.0 + scale_mod.astype(jnp.float32)) + shift.astype(jnp.float32)
    ).astype(jnp.bfloat16)
    embed = jnp.dot(
        hidden,
        lax.all_gather(head_weight, "gen", axis=0, tiled=True),
        preferred_element_type=jnp.float32,
    )
    length = jnp.sqrt(jnp.sum(embed * embed, axis=1, keepdims=True) + 1e-06)
    unit_exact = embed / length
    unit = unit_exact.astype(jnp.bfloat16)
    members = lax.all_gather(unit, "bank", axis=0, tiled=True)
    batch = members.shape[0]
    scores = jnp.dot(unit, members.T, preferred_element_type=jnp.float32)
    own_column = lax.axis_index("bank") * samples + lax.broadcasted_iota(jnp.int32, scores.shape, 0)
    same = lax.broadcasted_iota(jnp.int32, scores.shape, 1) == own_column
    pair_weight = jnp.where(same, jnp.float32(0.0), jnp.exp(kernel_scale * scores)).astype(
        jnp.bfloat16
    )
    near = jnp.dot(pair_weight, members, preferred_element_type=jnp.float32) / (batch - 1)
    bank_f = bank.astype(jnp.float32)
    bank_unit = (bank_f / jnp.sqrt(jnp.sum(bank_f * bank_f, axis=1, keepdims=True) + 1e-06)).astype(
        jnp.bfloat16
    )
    bank_scores = jnp.dot(members, bank_unit.T, preferred_element_type=jnp.float32)
    bank_weight = jnp.exp(kernel_scale * bank_scores).astype(jnp.bfloat16)
    far = lax.psum_scatter(
        jnp.dot(bank_weight, bank_unit, preferred_element_type=jnp.float32),
        "bank",
        scatter_dimension=0,
        tiled=True,
    ) / (bank.shape[0] * lax.axis_size("bank"))
    proof = near - far
    radial = jnp.sum(unit_exact * proof, axis=1, keepdims=True)
    grad_embed = ((proof - unit_exact * radial) / length).astype(jnp.bfloat16)
    feature_cols = lax.all_to_all(hidden, ("gen", "bank"), split_axis=1, concat_axis=0, tiled=True)
    every_grad = lax.all_gather(grad_embed, ("gen", "bank"), axis=0, tiled=True)
    gradient = lax.dot_general(
        feature_cols, every_grad, (((0,), (0,)), ((), ())), preferred_element_type=jnp.float32
    )
    squares = lax.psum(jnp.sum(gradient * gradient), ("gen", "bank"))
    entries = hidden.shape[1] * width
    return gradient * lax.rsqrt(squares / entries + 1e-06)


def solution(mesh):
    placed = (
        P(("gen", "bank"), None),
        P(("gen", "bank"), None),
        P(("gen", "bank"), None),
        P("gen", None),
        P("bank", None),
    )
    return jax.shard_map(
        local, mesh=mesh, in_specs=placed, out_specs=P(("gen", "bank"), None), check_vma=False
    )
```

profile of v0, /device:TPU:0, one launch (start us, length us, event | category | flops | bytes accessed | tf_op | source)
XLA Modules:
  0.0 311.0 jit_solution(15874247557174399582)
XLA Ops:
  6.5 0.0 all-gather.4.cloned.1.call-start
  6.5 0.7 all-gather.4.cloned.1.call-update
  7.3 0.0 all-gather.6.cloned.1.call-start
  7.3 1.2 fusion.6
  8.6 1.7 fusion.9
  10.2 59.7 %all-gather.4.cloned.1.call-done = bf16[4096,1024]{1,0:T(8,128)(2,1)} async-done(((bf16[1024,1024]{1,0:T(8,128)(2,1)}), bf16[4096,1024]{1,0:T(8,128)(2,1)}) %all-gather.4.cloned.1.call-update) | async-done | bytes 8388624 | tf_op jit(solution)/shard_map/all_gather | solution.py:19
  69.9 5.1 %multiply_reduce_fusion.2 = (f32[64]{0:T(128)S(1)}, f32[64,1024]{1,0:T(8,128)S(1)}) fusion(bf16[64,4096]{1,0:T(8,128)(2,1)S(1)} %fusion.9, bf16[4096,1024]{1,0:T(8,128)(2,1)} %all-gather.4.cloned.1.call-done), kind=kOutput, calls=%fused_computation.23 | convolution fusion | flops 537001920 | bytes 9175296 | tf_op jit(solution)/shard_map/dot_general | solution.py:17
  75.0 0.8 fusion.19
  75.7 0.0 all-gather.6.cloned.1.call-update
  75.8 0.0 reduce-scatter.2.cloned.1.call-start
  75.8 3.1 fusion
  78.9 37.3 %all-gather.6.cloned.1.call-done = bf16[512,1024]{1,0:T(8,128)(2,1)} async-done(((bf16[64,1024]{1,0:T(8,128)(2,1)}), bf16[512,1024]{1,0:T(8,128)(2,1)}) %all-gather.6.cloned.1.call-update) | async-done | bytes 1048592 | tf_op jit(solution)/shard_map/all_gather | solution.py:25
  116.2 0.0 copy-start
  116.2 9.8 %fusion.10 = f32[512,1024]{1,0:T(8,128)} fusion(bf16[512,1024]{1,0:T(8,128)(2,1)} %all-gather.6.cloned.1.call-done, bf16[2048,1024]{1,0:T(8,128)(2,1)} %param.9, f32[2048]{0:T(1024)S(1)} %add_sqrt_fusion), kind=kOutput, calls=%fused_computation.17 | convolution fusion | flops 4309647360 | bytes 7348224 | tf_op jit(solution)/shard_map/dot_general | solution.py:41
  126.0 0.0 reduce-scatter.2.cloned.1.call-update
  126.1 0.0 all-gather.8.cloned.1.call-start
  126.1 67.6 %reduce-scatter.2.cloned.1.call-done = f32[64,1024]{1,0:T(8,128)} async-done(((f32[512,1024]{1,0:T(8,128)}), f32[64,1024]{1,0:T(8,128)}) %reduce-scatter.2.cloned.1.call-update) | async-done | bytes 262160 | tf_op jit(solution)/shard_map/reduce_scatter | solution.py:40
  193.8 0.0 copy-done
  193.8 1.8 multiply_reduce_fusion.1
  195.6 0.8 divide_convert_fusion
  196.3 0.0 all-gather.8.cloned.1.call-update
  196.4 0.1 copy_bitcast_fusion
  196.5 22.3 %all_to_all.19 = bf16[64,32,128]{2,0,1:T(8,128)(2,1)S(1)} all-to-all(bf16[64,32,128]{2,0,1:T(8,128)(2,1)S(1)} %copy_bitcast_fusion), channel_id=1, replica_groups=mesh['gen'=4,'bank'=8] {'gen','bank'}, dimensions={1} | all-to-all | bytes 1048576 | tf_op jit(solution)/shard_map/all_to_all | solution.py:49
  218.8 41.3 %all-gather.8.cloned.1.call-done = bf16[2048,1024]{1,0:T(8,128)(2,1)} async-done(((bf16[64,1024]{1,0:T(8,128)(2,1)}), bf16[2048,1024]{1,0:T(8,128)(2,1)}) %all-gather.8.cloned.1.call-update) | async-done | bytes 4194320 | tf_op jit(solution)/shard_map/all_gather | solution.py:50
  260.1 3.6 %multiply_reduce_fusion = (f32[]{:T(128)}, f32[128,1024]{1,0:T(8,128)S(1)}) fusion(bf16[2048,128]{1,0:T(8,128)(2,1)S(1)} %bitcast.15, bf16[2048,1024]{1,0:T(8,128)(2,1)} %all-gather.8.cloned.1.call-done), kind=kOutput, calls=%fused_computation.19 | convolution fusion | flops 537133056 | bytes 5242884 | tf_op jit(solution)/shard_map/dot_general | solution.py:51
  263.7 39.3 %psum.7 = f32[]{:T(128)} all-reduce(f32[]{:T(128)} %get-tuple-element.9), channel_id=1, replica_groups=mesh['gen'=4,'bank'=8] {'gen','bank'}, use_global_device_ids=true, to_apply=%region_6.7 | all-reduce | flops 1 | bytes 8 | tf_op jit(solution)/shard_map/psum | solution.py:54
  303.7 0.8 broadcast_multiply_fusion
  (4 shorter events, 0.0 us)
Async XLA Ops:
  6.5 63.4 %all-gather.4.cloned.1.call-start = ((), (), s32[]{:S(2)}) async-start(), calls=%async_computation.2 | async-start | bytes 10485760 | tf_op jit(solution)/shard_map/all_gather | solution.py:19
  7.3 108.9 %all-gather.6.cloned.1.call-start = ((), (), s32[]{:S(2)}) async-start(), calls=%async_computation.3 | async-start | bytes 1179648 | tf_op jit(solution)/shard_map/all_gather | solution.py:25
  75.8 118.0 %reduce-scatter.2.cloned.1.call-start = ((), (), s32[]{:S(2)}) async-start(), calls=%async_computation.4 | async-start | bytes 2359296 | tf_op jit(solution)/shard_map/reduce_scatter | solution.py:40
  116.2 77.6 %copy-start = (bf16[512,1024]{1,0:T(8,128)(2,1)S(1)}, bf16[512,1024]{1,0:T(8,128)(2,1)}, u32[]{:S(2)}) copy-start(bf16[512,1024]{1,0:T(8,128)(2,1)} %all-gather.6.cloned.1.call-done) | copy-start | bytes 3145732
  126.1 134.0 %all-gather.8.cloned.1.call-start = ((), (), s32[]{:S(2)}) async-start(), calls=%async_computation.5 | async-start | bytes 4325376 | tf_op jit(solution)/shard_map/all_gather | solution.py:50
Sparse Core Ops, SparseCore 0:
  8.9 60.9 all-gather.3
  75.9 40.2 all-gather.5
  126.2 67.5 reduce-scatter.1
  196.7 63.3 all-gather.7
where the time goes:
time: 311 us
  waiting for transfers between devices  207 us (67%)
  blocking collectives  61.6 us (20%)
  matrix products  20.3 us (7%)
  between operations  13.9 us (4%)
  other arithmetic  8.39 us (3%)
    reduce_scatter x1, waiting for transfers between devices, local(): lax.psum_scatter(jnp.dot(bank_weight, bank_unit, preferred_element_type=j...  67.6 us
    all_gather x1, waiting for transfers between devices, local(): lax.all_gather(head_weight, 'gen', axis=0, tiled=True)  59.7 us
    all_gather x1, waiting for transfers between devices, local(): every_grad = lax.all_gather(grad_embed, ('gen', 'bank'), axis=0, tiled=True)  41.3 us
    psum x1, blocking collectives, local(): squares = lax.psum(jnp.sum(gradient * gradient), ('gen', 'bank'))  39.3 us
    all_gather x1, waiting for transfers between devices, local(): members = lax.all_gather(unit, 'bank', axis=0, tiled=True)  37.3 us
    all_to_all x1, blocking collectives, local(): lax.all_to_all(hidden, ('gen', 'bank'), split_axis=1, concat_axis=0, tile...  22.3 us
    dot_general x1, matrix products, local(): jnp.dot(bank_weight, bank_unit, preferred_element_type=jnp.float32)  9.83 us
  transfers between devices with their start and end apart: 4, of which 4 were waited for; matrix products, arithmetic and copies ran while one was open for 2% of the time, Pallas kernels for 0%

commit v1 on v0

v1 whole, which is shorter than its diff:
```python
import jax
import jax.numpy as jnp
from jax import lax
from jax.experimental import pallas as pl
from jax.experimental.pallas import tpu as pltpu
from jax.sharding import PartitionSpec as P

kernel_scale = 32.0
F32, BF16 = jnp.float32, jnp.bfloat16
SMEM = pl.BlockSpec(memory_space=pltpu.SMEM)
VMEM = pl.BlockSpec(memory_space=pltpu.VMEM)
HBM = pl.BlockSpec(memory_space=pltpu.HBM)


def swap(value, axis, mask):
    count = lax.axis_size(axis)
    return lax.ppermute(value, axis, [(i, i ^ mask) for i in range(count)])


def call(body, scalars, arrays, outs, flops, scratch=(), to_hbm=False, from_hbm=False):
    space = pltpu.HBM if from_hbm else pltpu.VMEM
    arrays = [pltpu.with_memory_space_constraint(a, space) for a in arrays]
    make = jax.ShapeDtypeStruct if to_hbm else pltpu.VMEM
    size = sum(a.size * a.dtype.itemsize for a in arrays)
    head = [] if scalars is None else [scalars]
    return pl.pallas_call(
        body,
        in_specs=[SMEM] * len(head) + [HBM if from_hbm else VMEM] * len(arrays),
        out_specs=[VMEM] * len(outs),
        out_shape=[make(dims, dtype) for dims, dtype in outs],
        scratch_shapes=list(scratch),
        compiler_params=pltpu.CompilerParams(vmem_limit_bytes=24 << 20),
        cost_estimate=pl.CostEstimate(flops=flops, bytes_accessed=size, transcendentals=0),
    )(*head, *arrays)


def modulate(place, latents, shift, scale_mod):
    samples, depth = latents.shape
    rows = 16
    quarter = depth // 4
    steps = samples // rows

    def body(place, x_hbm, b_hbm, s_hbm, hid_ref, lent_ref, own_ref, x_ref, b_ref, s_ref, sems):
        side, core = place[0], place[1]
        copies = [
            [
                pltpu.make_async_copy(src.at[pl.ds(r * rows, rows)], dst.at[r], sems.at[i, r])
                for i, (src, dst) in enumerate(
                    ((x_hbm, x_ref), (b_hbm, b_ref), (s_hbm, s_ref))
                )
            ]
            for r in range(steps)
        ]
        for group in copies:
            for copy in group:
                copy.start()
        for r in range(steps):
            for copy in copies[r]:
                copy.wait()
            at = slice(r * rows, (r + 1) * rows)
            x = x_ref[r].astype(F32)
            inverse = lax.rsqrt(jnp.mean(x * x, axis=1, keepdims=True) + 1e-06)
            hid_ref[at] = (
                x * inverse * (1.0 + s_ref[r].astype(F32)) + b_ref[r].astype(F32)
            ).astype(BF16)
        for ref, s in ((lent_ref, 1 - side), (own_ref, side)):
            for i, c in enumerate((core, 1 - core)):
                start = pl.multiple_of((2 * s + c) * quarter, quarter)
                ref[:, i * quarter : (i + 1) * quarter] = hid_ref[:, pl.ds(start, quarter)]

    half = (samples, depth // 2)
    return call(
        body,
        place,
        [latents, shift, scale_mod],
        [((samples, depth), BF16), (half, BF16), (half, BF16)],
        8 * samples * depth,
        [pltpu.VMEM((steps, rows, depth), BF16)] * 3 + [pltpu.SemaphoreType.DMA((3, steps))],
        from_hbm=True,
    )


def project(block, first, second):
    samples = block.shape[0]
    quarter, width = first.shape

    def body(x_ref, w_ref, v_ref, o_ref):
        o_ref[...] = jnp.dot(
            x_ref[:, :quarter], w_ref[...], preferred_element_type=F32
        ) + jnp.dot(x_ref[:, quarter:], v_ref[...], preferred_element_type=F32)

    return call(
        body, None, [block, first, second], [((samples, width), F32)], 4 * samples * quarter * width
    )[0]


def finish_embed(part, other):
    def body(a_ref, b_ref, exact_ref, unit_ref, length_ref):
        embed = a_ref[...] + b_ref[...].astype(F32)
        length = jnp.sqrt(jnp.sum(embed * embed, axis=1, keepdims=True) + 1e-06)
        exact = embed / length
        exact_ref[...] = exact
        unit_ref[...] = exact.astype(BF16)
        length_ref[...] = jnp.broadcast_to(length, length_ref.shape)

    samples, width = part.shape
    return call(
        body,
        None,
        [part, other],
        [((samples, width), F32), ((samples, width), BF16), ((samples, 128), F32)],
        6 * samples * width,
    )


def shares(rows):
    return 9 * rows // 64, 14 * rows // 64


def prepare(place, bank, weight):
    rows, width = bank.shape
    steps = 8
    tile = rows // steps
    forward, direct = shares(rows)

    def body(place, x_hbm, w_hbm, o_ref, f_ref, d_ref, w_ref, x_ref, sems):
        copies = [
            pltpu.make_async_copy(x_hbm.at[pl.ds(i * tile, tile)], x_ref.at[i], sems.at[i])
            for i in range(steps)
        ] + [pltpu.make_async_copy(w_hbm, w_ref, sems.at[steps])]
        for copy in copies:
            copy.start()
        for i in range(steps):
            copies[i].wait()
            x = x_ref[i].astype(F32)
            o_ref[i * tile : (i + 1) * tile] = (
                x / jnp.sqrt(jnp.sum(x * x, axis=1, keepdims=True) + 1e-06)
            ).astype(BF16)
        start = pl.multiple_of((2 * place[0] + place[1]) * forward, 16)
        f_ref[...] = o_ref[pl.ds(start, forward), :]
        start = pl.multiple_of(4 * forward + place[1] * direct, 16)
        d_ref[...] = o_ref[pl.ds(start, direct), :]
        copies[steps].wait()

    return call(
        body,
        place,
        [bank, weight],
        [
            (bank.shape, BF16),
            ((forward, width), BF16),
            ((direct, width), BF16),
            (weight.shape, BF16),
        ],
        8 * bank.size,
        [pltpu.VMEM((steps, tile, width), BF16), pltpu.SemaphoreType.DMA((steps + 1,))],
        from_hbm=True,
    )


def join(pieces):
    samples, width = pieces[0].shape
    count = len(pieces)

    def body(*refs):
        for i in range(count):
            refs[-1][i * samples : (i + 1) * samples] = refs[i][...]

    return call(body, None, pieces, [((count * samples, width), BF16)], 0)[0]


def bank_sums(line, blocks, before=None, samples=None):
    total, width = line.shape
    count = 1 if samples is None else total // samples

    def body(*refs):
        line_ref, rest = refs[0], refs[1:]
        row_refs, rest = rest[: len(blocks)], rest[len(blocks) :]
        outs, sums = rest[-1 - count : -1], rest[-1]
        started = before is not None
        if started:
            sums[...] = rest[0][...]
        for block, ref in zip(blocks, row_refs):
            tile = min(512, block.shape[0])
            for start in range(0, block.shape[0], tile):
                rows = ref[start : start + tile]
                scores = lax.dot_general(
                    line_ref[...], rows, (((1,), (1,)), ((), ())), preferred_element_type=F32
                )
                weight = jnp.exp(kernel_scale * scores).astype(BF16)
                term = jnp.dot(weight, rows, preferred_element_type=F32)
                sums[...] = sums[...] + term if started else term
                started = True
        for i, ref in enumerate(outs):
            size = total // count
            ref[...] = sums[i * size : (i + 1) * size].astype(ref.dtype)

    dims = (total // count, width)
    return call(
        body,
        None,
        [line] + list(blocks) + ([] if before is None else [before]),
        [(dims, BF16 if i else F32) for i in range(count)],
        4 * total * width * sum(block.shape[0] for block in blocks),
        [pltpu.VMEM((total, width), F32)],
    )


def pair_sums(unit, line, across):
    samples, width = unit.shape
    batch = 2 * line.shape[0]

    def body(unit_ref, line_ref, across_ref, out_ref):
        total = 0.0
        for ref, first in ((line_ref, True), (across_ref, False)):
            scores = lax.dot_general(
                unit_ref[...], ref[...], (((1,), (1,)), ((), ())), preferred_element_type=F32
            )
            weight = jnp.exp(kernel_scale * scores)
            if first:
                same = lax.broadcasted_iota(
                    jnp.int32, scores.shape, 0
                ) == lax.broadcasted_iota(jnp.int32, scores.shape, 1)
                weight = jnp.where(same, 0.0, weight)
            total = total + jnp.dot(
                weight.astype(BF16), ref[...], preferred_element_type=F32
            )
        out_ref[...] = total / (batch - 1)

    return call(
        body, None, [unit, line, across], [((samples, width), F32)], 4 * samples * width * batch
    )[0]


def embed_gradient(near, far, parts, exact, length, bank_rows):
    count = len(parts)

    def body(*refs):
        near_ref, far_ref, exact_ref, length_ref = refs[:4]
        total = far_ref[...]
        for ref in refs[4 : 4 + count]:
            total = total + ref[...].astype(F32)
        proof = near_ref[...] - total / bank_rows
        exact = exact_ref[...]
        radial = jnp.sum(exact * proof, axis=1, keepdims=True)
        refs[-1][...] = ((proof - exact * radial) / length_ref[:, :1]).astype(BF16)

    samples, width = near.shape
    return call(
        body,
        None,
        [near, far, exact, length] + list(parts),
        [((samples, width), BF16)],
        (count + 8) * samples * width,
    )[0]


def spread(place, hidden, n_bank):
    samples, depth = hidden.shape
    pair = depth // 4 // n_bank * 2

    def body(place, hid_ref, *outs):
        for i, ref in enumerate(outs):
            for g in range(4):
                start = pl.multiple_of(g * (depth // 4) + (place[2] ^ i) * pair, pair)
                ref[:, g * pair : (g + 1) * pair] = hid_ref[:, pl.ds(start, pair)]

    return call(body, place, [hidden], [((samples, 4 * pair), BF16)] * (n_bank // 2), 0)


def split_pairs(place, pieces):
    samples, width = pieces[0].shape
    block = width // 8
    count = len(pieces)

    def body(place, *refs):
        ins, outs = refs[:count], refs[count:]
        for out, y in zip(outs, (place[3], 1 - place[3])):
            for i, ref in enumerate(ins):
                for g in range(4):
                    start = pl.multiple_of((2 * g + y) * block, block)
                    out[i * samples : (i + 1) * samples, g * block : (g + 1) * block] = ref[
                        :, pl.ds(start, block)
                    ]

    return call(body, place, pieces, [((count * samples, 4 * block), BF16)] * 2, 0)


def turn(kept, given):
    rows, width = kept.shape

    def body(a_ref, b_ref, o_ref):
        o_ref[:, :rows] = a_ref[...].T
        o_ref[:, rows:] = b_ref[...].T

    return call(body, None, [kept, given], [((width, 2 * rows), BF16)], 0)[0]


def feature_sums(place, columns, grads, away):
    samples, width = grads[0].shape
    count = len(grads)
    piece = columns.shape[0] // 4

    def body(place, cols_ref, *refs):
        ins, outs, held = refs[:count], refs[count : count + 2], refs[-1]
        side, core = place[0], place[1]
        for i in range(count):
            held[i * samples : (i + 1) * samples] = ins[i][...]
        s = 1 - side if away else side
        for ref, c in zip(outs, (1 - core, core)):
            start = pl.multiple_of((2 * s + c) * piece, piece)
            ref[...] = jnp.dot(
                cols_ref[pl.ds(start, piece), :], held[...], preferred_element_type=F32
            )

    return call(
        body,
        place,
        [columns] + list(grads),
        [((piece, width), F32)] * 2,
        4 * piece * width * count * samples,
        [pltpu.VMEM((count * samples, width), BF16)],
    )


def add_round(a, b):
    def body(a_ref, b_ref, o_ref):
        o_ref[...] = (a_ref[...] + b_ref[...]).astype(BF16)

    return call(body, None, [a, b], [(a.shape, BF16)], a.size)[0]


def square_sums(kept, from_core, from_side, devices):
    rows, width = kept.shape

    def body(a_ref, b_ref, c_ref, grad_ref, out_ref):
        grad = a_ref[...] + b_ref[...] + c_ref[...].astype(F32)
        grad_ref[...] = grad
        squares = jnp.sum((grad * grad).reshape(rows // 8, 8, width), axis=0)
        tile = squares[:, :128]
        for i in range(1, width // 128):
            tile = tile + squares[:, i * 128 : (i + 1) * 128]
        out_ref[...] = jnp.broadcast_to(tile[None], out_ref.shape)

    return call(
        body,
        None,
        [kept, from_core, from_side],
        [((rows, width), F32), ((devices, 8, 128), F32)],
        4 * rows * width,
    )


def scaled(gradient, squares, entries):
    def body(g_ref, s_ref, o_ref):
        mean = jnp.sum(s_ref[...]) / entries
        o_ref[...] = g_ref[...] * lax.rsqrt(jnp.full((1, 1), mean + 1e-06, F32))

    return call(
        body, None, [gradient, squares], [(gradient.shape, F32)], gradient.size, (), True
    )[0]


def by_feature(place, hidden, n_bank):
    samples, depth = hidden.shape
    piece = depth // 4 // n_bank
    if piece % 128 == 0:
        pieces = spread(place, hidden, n_bank)
        pieces = [swap(p, "bank", 2 * i) if i else p for i, p in enumerate(pieces)]
        kept, given = split_pairs(place, pieces)
        return turn(kept, swap(given, "bank", 1))
    pairs = hidden.reshape(samples, 4, n_bank // 2, 2 * piece)
    pieces = [
        lax.dynamic_index_in_dim(pairs, place[2] ^ i, 2, keepdims=False)
        for i in range(n_bank // 2)
    ]
    pieces = [swap(p, "bank", 2 * i) if i else p for i, p in enumerate(pieces)]
    columns = jnp.concatenate(pieces, 0)
    kept = lax.dynamic_slice_in_dim(columns, place[3] * piece, piece, 2)
    given = swap(lax.dynamic_slice_in_dim(columns, (1 - place[3]) * piece, piece, 2), "bank", 1)
    return jnp.concatenate([kept, given], 0).reshape(n_bank * samples, 4 * piece).T


def local(latents, shift, scale_mod, head_weight, bank):
    samples, depth = latents.shape
    width = head_weight.shape[1]
    n_gen = lax.axis_size("gen")
    n_bank = lax.axis_size("bank")
    gen = lax.axis_index("gen")
    me = lax.axis_index("bank")
    place = jnp.stack([gen // 2, gen % 2, me // 2, me % 2]).astype(jnp.int32)
    evens, odds = list(range(0, n_bank, 2)), list(range(1, n_bank, 2))

    head_other = swap(head_weight, "gen", 1)
    hidden, lent, own = modulate(place, latents, shift, scale_mod)
    bank, head_weight, lent = lax.optimization_barrier((bank, head_weight, lent))
    lent = swap(lent, "gen", 2)
    bank_unit, forward, direct, head_weight = prepare(place, bank, head_weight)
    own_part = project(own, head_weight, head_other)
    returned = swap(project(lent, head_weight, head_other), "gen", 2)
    exact, unit, length = finish_embed(own_part, returned)

    columns = by_feature(place, hidden, n_bank)

    forward = swap(forward, "bank", 1)
    direct = swap(direct, "bank", 1)
    beside = swap(forward, "gen", 2)
    early = [forward, swap(forward, "gen", 1)]
    late = [beside, direct]
    late += [swap(v, "gen", 1) for v in late]

    line = [unit] + [swap(unit, "bank", m) for m in evens[1:]]
    line = join(line)
    across = swap(line, "bank", 1)
    sums = bank_sums(line, [bank_unit])[0]
    sums = bank_sums(line, early, sums)[0]
    far = bank_sums(line, late, sums, samples)
    parts = [swap(v, "bank", m) for m, v in zip(evens[1:], far[1:])]
    near = pair_sums(unit, line, across)
    grad_embed = embed_gradient(near, far[0], parts, exact, length, bank.shape[0] * n_bank)

    grads = {0: grad_embed}
    for m in range(n_bank - 1, 0, -1):
        grads[m] = swap(grad_embed, "bank", m)
    grads = [grads[m] for m in evens + odds]
    for_core, ours = feature_sums(place, columns, grads, True)
    away = add_round(ours, swap(for_core, "gen", 1))
    for_core, ours = feature_sums(place, columns, grads, False)
    gradient, squares = square_sums(
        ours, swap(for_core, "gen", 1), swap(away, "gen", 2), n_gen * n_bank
    )
    squares = lax.all_to_all(squares, ("gen", "bank"), 0, 0, tiled=True)
    return scaled(gradient, squares, depth * width)


def solution(mesh):
    placed = (
        P(("gen", "bank"), None),
        P(("gen", "bank"), None),
        P(("gen", "bank"), None),
        P("gen", None),
        P("bank", None),
    )
    return jax.shard_map(
        lambda *args: local(*args),
        mesh=mesh,
        in_specs=placed,
        out_specs=P(("gen", "bank"), None),
        check_vma=False,
    )
```

time: 311 us -> 167 us (0.54)
  waiting for transfers between devices: 207 us -> 92.7 us
  blocking collectives: 61.6 us -> 10.5 us
  starting transfers between devices: 0.12 us -> 42.9 us
  matrix products: 20.3 us -> 0 us
  Pallas kernels: 0 us -> 20.2 us
  between operations: 13.9 us -> 0.22 us
  other arithmetic: 8.39 us -> 0.08 us
    all_gather x3 -> x0, waiting for transfers between devices: 138 us -> none  [the longest x1 59.7 us: local(): lax.all_gather(head_weight, 'gen', axis=0, tiled=True)]
    ppermute x0 -> x30, waiting for transfers between devices: none -> 92.7 us  [swap(): return lax.ppermute(value, axis, [(i, i ^ mask) for i in range(count)])]
    reduce_scatter x1 -> x0, waiting for transfers between devices: 67.6 us -> none  [local(): lax.psum_scatter(jnp.dot(bank_weight, bank_unit, preferred_element_type=j...]
    ppermute x0 -> x30, starting transfers between devices: none -> 42.9 us  [swap(): return lax.ppermute(value, axis, [(i, i ^ mask) for i in range(count)])]
    psum x1 -> x0, blocking collectives: 39.3 us -> none  [local(): squares = lax.psum(jnp.sum(gradient * gradient), ('gen', 'bank'))]
    dot_general x4 -> x0, matrix products: 20.3 us -> none  [the longest x1 9.83 us: local(): jnp.dot(bank_weight, bank_unit, preferred_element_type=jnp.float32)]
    pallas_call x0 -> x19, Pallas kernels: none -> 20.2 us  [call(): pl.pallas_call(body, in_specs=[SMEM] * len(head) + [HBM if from_hbm else...]
    all_to_all x1, blocking collectives: 22.3 us -> 10.5 us  [local(): squares = lax.all_to_all(squares, ('gen', 'bank'), 0, 0, tiled=True)]
  transfers between devices with their start and end apart: 4 -> 30, of which waited for: 4 -> 14; matrix products, arithmetic and copies ran while one was open for 2% -> 0% of each run, Pallas kernels for 0% -> 11%
where the time goes in v1:
time: 167 us
  waiting for transfers between devices  92.7 us (56%)
  starting transfers between devices  42.9 us (26%)
  Pallas kernels  20.2 us (12%)
  blocking collectives  10.5 us (6%)
    ppermute x30, waiting for transfers between devices, swap(): return lax.ppermute(value, axis, [(i, i ^ mask) for i in range(count)])  92.7 us
    ppermute x30, starting transfers between devices, swap(): return lax.ppermute(value, axis, [(i, i ^ mask) for i in range(count)])  42.9 us
    pallas_call x19, Pallas kernels, call(): pl.pallas_call(body, in_specs=[SMEM] * len(head) + [HBM if from_hbm else...  20.2 us
    all_to_all x1, blocking collectives, local(): squares = lax.all_to_all(squares, ('gen', 'bank'), 0, 0, tiled=True)  10.5 us
  transfers between devices with their start and end apart: 30, of which 14 were waited for; matrix products, arithmetic and copies ran while one was open for 0% of the time, Pallas kernels for 11%

profile of v1, /device:TPU:0, one launch (start us, length us, event | category | flops | bytes accessed | tf_op | source)
XLA Modules:
  0.0 166.7 jit_solution(8998542607135849803)
XLA Ops:
  0.6 2.4 %shard_map.55 = (bf16[64,4096]{1,0:T(8,128)(2,1)S(1)}, bf16[64,2048]{1,0:T(8,128)(2,1)S(1)}, bf16[64,2048]{1,0:T(8,128)(2,1)S(1)}) custom-call(s32[4]{0:T(128)S(1)} %pad_add_fusion.place, bf16[64,4096]{1,0:T(8,128)(2,1)} %x_hbm.1, bf16[64,4096]{1,0:T(8,128)(2,1)} %b_hbm.1, bf16[64,4096]{1,0:T(8,128)(2,1)} %s_hbm.1), custom_call_target="tpu_custom_call" | custom-call | flops 2097152 | bytes 1572864 | tf_op jit(solution)/shard_map/pallas_call | solution.py:26
  3.0 3.5 %shard_map.59 = (bf16[2048,1024]{1,0:T(8,128)(2,1)S(1)}, bf16[288,1024]{1,0:T(8,128)(2,1)S(1)}, bf16[448,1024]{1,0:T(8,128)(2,1)S(1)}, bf16[1024,1024]{1,0:T(8,128)(2,1)S(1)}) custom-call(s32[4]{0:T(128)S(1)} %pad_add_fusion.place, bf16[2048,1024]{1,0:T(8,128)(2,1)} %x_hbm.2, bf16[1024,1024]{1,0:T(8,128)(2,1)} %w_hbm), custom_call_target="tpu_custom_call" | custom-call | flops 16777216 | bytes 6291456 | tf_op jit(solution)/shard_map/pallas_call | solution.py:26
  6.5 2.6 %collective-permute-start.13 = (bf16[448,1024]{1,0:T(8,128)(2,1)S(1)}, bf16[448,1024]{1,0:T(8,128)(2,1)S(1)}, u32[]{:S(2)}, u32[]{:S(2)}) collective-permute-start(bf16[448,1024]{1,0:T(8,128)(2,1)S(1)} %get-tuple-element.49), channel_id=1, source_target_pairs={{0,1},{1,0},{2,3},{3,2},{4,5},{5,4},{6,7},{7,6},{8,9},{9,8},{10,11... | collective-permute-start | bytes 2752520 | tf_op jit(solution)/shard_map/ppermute | solution.py:17
  9.1 33.6 %collective-permute-done.11.refs_1_ = bf16[288,1024]{1,0:T(8,128)(2,1)S(1)} collective-permute-done((bf16[288,1024]{1,0:T(8,128)(2,1)S(1)}, bf16[288,1024]{1,0:T(8,128)(2,1)S(1)}, u32[]{:S(2)}, u32[]{:S(2)}) %collective-permute-start.11) | collective-permute-done | bytes 589856 | tf_op jit(solution)/shard_map/ppermute | solution.py:17
  42.7 1.7 %collective-permute-start.12 = (bf16[288,1024]{1,0:T(8,128)(2,1)S(1)}, bf16[288,1024]{1,0:T(8,128)(2,1)S(1)}, u32[]{:S(2)}, u32[]{:S(2)}) collective-permute-start(bf16[288,1024]{1,0:T(8,128)(2,1)S(1)} %collective-permute-done.11.refs_1_), channel_id=1, source_target_pairs={{0,16},{8,24},{16,0},{24,8},{1,17},{9,25},{17,1},{25,9},{2,18},{10... | collective-permute-start | bytes 1769480 | tf_op jit(solution)/shard_map/ppermute | solution.py:17
  44.8 18.7 %collective-permute-done.5.x_ref = bf16[64,2048]{1,0:T(8,128)(2,1)S(1)} collective-permute-done((bf16[64,2048]{1,0:T(8,128)(2,1)S(1)}, bf16[64,2048]{1,0:T(8,128)(2,1)S(1)}, u32[]{:S(2)}, u32[]{:S(2)}) %collective-permute-start.5) | collective-permute-done | bytes 262176 | tf_op jit(solution)/shard_map/ppermute | solution.py:17
  64.4 1.5 collective-permute-start.6
  67.2 4.5 %collective-permute-done.6.b_ref = f32[64,1024]{1,0:T(8,128)S(1)} collective-permute-done((f32[64,1024]{1,0:T(8,128)S(1)}, f32[64,1024]{1,0:T(8,128)S(1)}, u32[]{:S(2)}, u32[]{:S(2)}) %collective-permute-start.6) | collective-permute-done | bytes 262176 | tf_op jit(solution)/shard_map/ppermute | solution.py:17
  71.8 3.3 %collective-permute-start.9 = (bf16[64,1024]{1,0:T(8,128)(2,1)S(1)}, bf16[64,1024]{1,0:T(8,128)(2,1)S(1)}, u32[]{:S(2)}, u32[]{:S(2)}) collective-permute-start(bf16[64,1024]{1,0:T(8,128)(2,1)S(1)} %get-tuple-element.47.refs_0_.unit_ref), channel_id=1, source_target_pairs={{0,6},{1,7},{2,4},{3,5},{4,2},{5,3},{6,0},{7,1},{8,14},{9,15},{10,... | collective-permute-start | bytes 393224 | tf_op jit(solution)/shard_map/ppermute | solution.py:17
  75.2 3.8 %collective-permute-done.9.refs_3_ = bf16[64,1024]{1,0:T(8,128)(2,1)S(1)} collective-permute-done((bf16[64,1024]{1,0:T(8,128)(2,1)S(1)}, bf16[64,1024]{1,0:T(8,128)(2,1)S(1)}, u32[]{:S(2)}, u32[]{:S(2)}) %collective-permute-start.9) | collective-permute-done | bytes 131104 | tf_op jit(solution)/shard_map/ppermute | solution.py:17
  79.0 4.5 %collective-permute-start.7 = (bf16[64,1024]{1,0:T(8,128)(2,1)S(1)}, bf16[64,1024]{1,0:T(8,128)(2,1)S(1)}, u32[]{:S(2)}, u32[]{:S(2)}) collective-permute-start(bf16[64,1024]{1,0:T(8,128)(2,1)S(1)} %get-tuple-element.47.refs_0_.unit_ref), channel_id=1, source_target_pairs={{0,2},{1,3},{2,0},{3,1},{4,6},{5,7},{6,4},{7,5},{8,10},{9,11},{10,... | collective-permute-start | bytes 393224 | tf_op jit(solution)/shard_map/ppermute | solution.py:17
  84.4 2.1 %collective-permute-done.7.refs_1_ = bf16[64,1024]{1,0:T(8,128)(2,1)S(1)} collective-permute-done((bf16[64,1024]{1,0:T(8,128)(2,1)S(1)}, bf16[64,1024]{1,0:T(8,128)(2,1)S(1)}, u32[]{:S(2)}, u32[]{:S(2)}) %collective-permute-start.7) | collective-permute-done | bytes 131104 | tf_op jit(solution)/shard_map/ppermute | solution.py:17
  86.5 2.1 %collective-permute-start.10 = (bf16[256,1024]{1,0:T(8,128)(2,1)S(1)}, bf16[256,1024]{1,0:T(8,128)(2,1)S(1)}, u32[]{:S(2)}, u32[]{:S(2)}) collective-permute-start(bf16[256,1024]{1,0:T(8,128)(2,1)S(1)} %shard_map.63.line_ref.refs_0_), channel_id=1, source_target_pairs={{0,1},{1,0},{2,3},{3,2},{4,5},{5,4},{6,7},{7,6},{8,9},{9,8},{10,11... | collective-permute-start | bytes 1572872 | tf_op jit(solution)/shard_map/ppermute | solution.py:17
  89.2 1.1 collective-permute-start
  90.3 2.7 %shard_map.65.refs_3_ = f32[256,1024]{1,0:T(8,128)S(1)} custom-call(bf16[256,1024]{1,0:T(8,128)(2,1)S(1)} %shard_map.63.line_ref.refs_0_, bf16[2048,1024]{1,0:T(8,128)(2,1)S(1)} %get-tuple-element.50.refs_1_), custom_call_target="tpu_custom_call" | custom-call | flops 2147483648 | bytes 4718592 | tf_op jit(solution)/shard_map/pallas_call | solution.py:26
  93.1 2.5 %collective-permute-start.1 = (bf16[64,1024]{1,0:T(8,128)(2,1)S(1)}, bf16[64,1024]{1,0:T(8,128)(2,1)S(1)}, u32[]{:S(2)}, u32[]{:S(2)}) collective-permute-start(bf16[64,1024]{1,0:T(8,128)(2,1)S(1)} %get-tuple-element.37), channel_id=1, source_target_pairs={{0,4},{1,5},{2,6},{3,7},{4,0},{5,1},{6,2},{7,3},{8,12},{9,13},{10,... | collective-permute-start | bytes 393224 | tf_op jit(solution)/shard_map/ppermute | solution.py:17
  95.6 1.5 shard_map.66.refs_5_
  97.1 1.5 collective-permute-start.2
  98.6 2.7 %shard_map.67 = (f32[64,1024]{1,0:T(8,128)S(1)}, bf16[64,1024]{1,0:T(8,128)(2,1)S(1)}, bf16[64,1024]{1,0:T(8,128)(2,1)S(1)}, bf16[64,1024]{1,0:T(8,128)(2,1)S(1)}) custom-call(bf16[256,1024]{1,0:T(8,128)(2,1)S(1)} %shard_map.63.line_ref.refs_0_, bf16[288,1024]{1,0:T(8,128)(2,1)S(1)} %collective-permute-done.12.refs_1_, ...), custom_call_target="tpu_custom_call" | custom-call | flops 1543503872 | bytes 4587520 | tf_op jit(solution)/shard_map/pallas_call | solution.py:26
  102.0 2.4 %collective-permute-start.18 = (bf16[64,1024]{1,0:T(8,128)(2,1)S(1)}, bf16[64,1024]{1,0:T(8,128)(2,1)S(1)}, u32[]{:S(2)}, u32[]{:S(2)}) collective-permute-start(bf16[64,1024]{1,0:T(8,128)(2,1)S(1)} %get-tuple-element.55), channel_id=1, source_target_pairs={{0,4},{1,5},{2,6},{3,7},{4,0},{5,1},{6,2},{7,3},{8,12},{9,13},{10,... | collective-permute-start | bytes 393224 | tf_op jit(solution)/shard_map/ppermute | solution.py:17
  104.4 3.8 %collective-permute-done.1.refs_2_ = bf16[64,1024]{1,0:T(8,128)(2,1)S(1)} collective-permute-done((bf16[64,1024]{1,0:T(8,128)(2,1)S(1)}, bf16[64,1024]{1,0:T(8,128)(2,1)S(1)}, u32[]{:S(2)}, u32[]{:S(2)}) %collective-permute-start.1) | collective-permute-done | bytes 131104 | tf_op jit(solution)/shard_map/ppermute | solution.py:17
  111.2 6.4 %collective-permute-done.18.refs_5_ = bf16[64,1024]{1,0:T(8,128)(2,1)S(1)} collective-permute-done((bf16[64,1024]{1,0:T(8,128)(2,1)S(1)}, bf16[64,1024]{1,0:T(8,128)(2,1)S(1)}, u32[]{:S(2)}, u32[]{:S(2)}) %collective-permute-start.18) | collective-permute-done | bytes 131104 | tf_op jit(solution)/shard_map/ppermute | solution.py:17
  118.0 5.2 %collective-permute-start.25 = (bf16[64,1024]{1,0:T(8,128)(2,1)S(1)}, bf16[64,1024]{1,0:T(8,128)(2,1)S(1)}, u32[]{:S(2)}, u32[]{:S(2)}) collective-permute-start(bf16[64,1024]{1,0:T(8,128)(2,1)S(1)} %shard_map.68.refs_0_), channel_id=1, source_target_pairs={{0,5},{1,4},{2,7},{3,6},{4,1},{5,0},{6,3},{7,2},{8,13},{9,12},{10,... | collective-permute-start | bytes 393224 | tf_op jit(solution)/shard_map/ppermute | solution.py:17
  123.2 1.4 collective-permute-start.23
  124.6 1.6 collective-permute-start.22
  126.9 6.8 %collective-permute-start.21 = (bf16[64,1024]{1,0:T(8,128)(2,1)S(1)}, bf16[64,1024]{1,0:T(8,128)(2,1)S(1)}, u32[]{:S(2)}, u32[]{:S(2)}) collective-permute-start(bf16[64,1024]{1,0:T(8,128)(2,1)S(1)} %shard_map.68.refs_0_), channel_id=1, source_target_pairs={{0,4},{1,5},{2,6},{3,7},{4,0},{5,1},{6,2},{7,3},{8,12},{9,13},{10,... | collective-permute-start | bytes 393224 | tf_op jit(solution)/shard_map/ppermute | solution.py:17
  133.8 4.9 %collective-permute-done.25.refs_6_ = bf16[64,1024]{1,0:T(8,128)(2,1)S(1)} collective-permute-done((bf16[64,1024]{1,0:T(8,128)(2,1)S(1)}, bf16[64,1024]{1,0:T(8,128)(2,1)S(1)}, u32[]{:S(2)}, u32[]{:S(2)}) %collective-permute-start.25) | collective-permute-done | bytes 131104 | tf_op jit(solution)/shard_map/ppermute | solution.py:17
  138.9 4.7 %collective-permute-done.20.refs_1_ = bf16[64,1024]{1,0:T(8,128)(2,1)S(1)} collective-permute-done((bf16[64,1024]{1,0:T(8,128)(2,1)S(1)}, bf16[64,1024]{1,0:T(8,128)(2,1)S(1)}, u32[]{:S(2)}, u32[]{:S(2)}) %collective-permute-start.20) | collective-permute-done | bytes 131104 | tf_op jit(solution)/shard_map/ppermute | solution.py:17
  144.7 1.0 shard_map.69
  146.7 1.1 collective-permute-done.27.b_ref
  147.8 7.3 %collective-permute-done.29.c_ref = bf16[128,1024]{1,0:T(8,128)(2,1)S(1)} collective-permute-done((bf16[128,1024]{1,0:T(8,128)(2,1)S(1)}, bf16[128,1024]{1,0:T(8,128)(2,1)S(1)}, u32[]{:S(2)}, u32[]{:S(2)}) %collective-permute-start.29) | collective-permute-done | bytes 262176 | tf_op jit(solution)/shard_map/ppermute | solution.py:17
  155.2 10.5 %all_to_all.5.s_ref = f32[32,8,128]{2,1,0:T(8,128)S(1)} all-to-all(f32[32,8,128]{2,1,0:T(8,128)S(1)} %get-tuple-element.62), channel_id=1, replica_groups=mesh['gen'=4,'bank'=8] {'gen','bank'}, dimensions={0} | all-to-all | bytes 262144 | tf_op jit(solution)/shard_map/all_to_all | solution.py:432
  (49 shorter events, 13.0 us)
Async XLA Ops:
  0.0 63.5 %collective-permute-start.4 = (bf16[1024,1024]{1,0:T(8,128)(2,1)}, bf16[1024,1024]{1,0:T(8,128)(2,1)S(1)}, u32[]{:S(2)}, u32[]{:S(2)}) collective-permute-start(bf16[1024,1024]{1,0:T(8,128)(2,1)} %w_hbm), channel_id=1, source_target_pairs={{0,8},{8,0},{16,24},{24,16},{1,9},{9,1},{17,25},{25,17},{2,10},{10... | collective-permute-start | bytes 6291464 | tf_op jit(solution)/shard_map/ppermute | solution.py:17
  6.5 38.3 %collective-permute-start.13 = (bf16[448,1024]{1,0:T(8,128)(2,1)S(1)}, bf16[448,1024]{1,0:T(8,128)(2,1)S(1)}, u32[]{:S(2)}, u32[]{:S(2)}) collective-permute-start(bf16[448,1024]{1,0:T(8,128)(2,1)S(1)} %get-tuple-element.49), channel_id=1, source_target_pairs={{0,1},{1,0},{2,3},{3,2},{4,5},{5,4},{6,7},{7,6},{8,9},{9,8},{10,11... | collective-permute-start | bytes 2752520 | tf_op jit(solution)/shard_map/ppermute | solution.py:17
  9.1 33.7 %collective-permute-start.11 = (bf16[288,1024]{1,0:T(8,128)(2,1)S(1)}, bf16[288,1024]{1,0:T(8,128)(2,1)S(1)}, u32[]{:S(2)}, u32[]{:S(2)}) collective-permute-start(bf16[288,1024]{1,0:T(8,128)(2,1)S(1)} %get-tuple-element.48), channel_id=1, source_target_pairs={{0,1},{1,0},{2,3},{3,2},{4,5},{5,4},{6,7},{7,6},{8,9},{9,8},{10,11... | collective-permute-start | bytes 1769480 | tf_op jit(solution)/shard_map/ppermute | solution.py:17
  42.7 23.1 %collective-permute-start.12 = (bf16[288,1024]{1,0:T(8,128)(2,1)S(1)}, bf16[288,1024]{1,0:T(8,128)(2,1)S(1)}, u32[]{:S(2)}, u32[]{:S(2)}) collective-permute-start(bf16[288,1024]{1,0:T(8,128)(2,1)S(1)} %collective-permute-done.11.refs_1_), channel_id=1, source_target_pairs={{0,16},{8,24},{16,0},{24,8},{1,17},{9,25},{17,1},{25,9},{2,18},{10... | collective-permute-start | bytes 1769480 | tf_op jit(solution)/shard_map/ppermute | solution.py:17
  44.4 19.1 %collective-permute-start.5 = (bf16[64,2048]{1,0:T(8,128)(2,1)S(1)}, bf16[64,2048]{1,0:T(8,128)(2,1)S(1)}, u32[]{:S(2)}, u32[]{:S(2)}) collective-permute-start(bf16[64,2048]{1,0:T(8,128)(2,1)S(1)} %get-tuple-element.46), channel_id=1, source_target_pairs={{0,16},{8,24},{16,0},{24,8},{1,17},{9,25},{17,1},{25,9},{2,18},{10... | collective-permute-start | bytes 786440 | tf_op jit(solution)/shard_map/ppermute | solution.py:17
  44.8 53.8 %collective-permute-start.15 = (bf16[448,1024]{1,0:T(8,128)(2,1)S(1)}, bf16[448,1024]{1,0:T(8,128)(2,1)S(1)}, u32[]{:S(2)}, u32[]{:S(2)}) collective-permute-start(bf16[448,1024]{1,0:T(8,128)(2,1)S(1)} %collective-permute-done.13.refs_2_), channel_id=1, source_target_pairs={{0,8},{8,0},{16,24},{24,16},{1,9},{9,1},{17,25},{25,17},{2,10},{10... | collective-permute-start | bytes 2752520 | tf_op jit(solution)/shard_map/ppermute | solution.py:17
  64.4 7.3 %collective-permute-start.6 = (f32[64,1024]{1,0:T(8,128)S(1)}, f32[64,1024]{1,0:T(8,128)S(1)}, u32[]{:S(2)}, u32[]{:S(2)}) collective-permute-start(f32[64,1024]{1,0:T(8,128)S(1)} %shard_map.61), channel_id=1, source_target_pairs={{0,16},{8,24},{16,0},{24,8},{1,17},{9,25},{17,1},{25,9},{2,18},{10... | collective-permute-start | bytes 786440 | tf_op jit(solution)/shard_map/ppermute | solution.py:17
  65.9 27.2 %collective-permute-start.16 = (bf16[288,1024]{1,0:T(8,128)(2,1)S(1)}, bf16[288,1024]{1,0:T(8,128)(2,1)S(1)}, u32[]{:S(2)}, u32[]{:S(2)}) collective-permute-start(bf16[288,1024]{1,0:T(8,128)(2,1)S(1)} %collective-permute-done.11.refs_1_), channel_id=1, source_target_pairs={{0,8},{8,0},{16,24},{24,16},{1,9},{9,1},{17,25},{25,17},{2,10},{10... | collective-permute-start | bytes 1769480 | tf_op jit(solution)/shard_map/ppermute | solution.py:17
  65.9 31.2 %collective-permute-start.14 = (bf16[288,1024]{1,0:T(8,128)(2,1)S(1)}, bf16[288,1024]{1,0:T(8,128)(2,1)S(1)}, u32[]{:S(2)}, u32[]{:S(2)}) collective-permute-start(bf16[288,1024]{1,0:T(8,128)(2,1)S(1)} %collective-permute-done.12.refs_1_), channel_id=1, source_target_pairs={{0,8},{8,0},{16,24},{24,16},{1,9},{9,1},{17,25},{25,17},{2,10},{10... | collective-permute-start | bytes 1769480 | tf_op jit(solution)/shard_map/ppermute | solution.py:17
  71.8 7.1 %collective-permute-start.9 = (bf16[64,1024]{1,0:T(8,128)(2,1)S(1)}, bf16[64,1024]{1,0:T(8,128)(2,1)S(1)}, u32[]{:S(2)}, u32[]{:S(2)}) collective-permute-start(bf16[64,1024]{1,0:T(8,128)(2,1)S(1)} %get-tuple-element.47.refs_0_.unit_ref), channel_id=1, source_target_pairs={{0,6},{1,7},{2,4},{3,5},{4,2},{5,3},{6,0},{7,1},{8,14},{9,15},{10,... | collective-permute-start | bytes 393224 | tf_op jit(solution)/shard_map/ppermute | solution.py:17
  75.2 9.2 %collective-permute-start.8 = (bf16[64,1024]{1,0:T(8,128)(2,1)S(1)}, bf16[64,1024]{1,0:T(8,128)(2,1)S(1)}, u32[]{:S(2)}, u32[]{:S(2)}) collective-permute-start(bf16[64,1024]{1,0:T(8,128)(2,1)S(1)} %get-tuple-element.47.refs_0_.unit_ref), channel_id=1, source_target_pairs={{0,4},{1,5},{2,6},{3,7},{4,0},{5,1},{6,2},{7,3},{8,12},{9,13},{10,... | collective-permute-start | bytes 393224 | tf_op jit(solution)/shard_map/ppermute | solution.py:17
  79.0 7.5 %collective-permute-start.7 = (bf16[64,1024]{1,0:T(8,128)(2,1)S(1)}, bf16[64,1024]{1,0:T(8,128)(2,1)S(1)}, u32[]{:S(2)}, u32[]{:S(2)}) collective-permute-start(bf16[64,1024]{1,0:T(8,128)(2,1)S(1)} %get-tuple-element.47.refs_0_.unit_ref), channel_id=1, source_target_pairs={{0,2},{1,3},{2,0},{3,1},{4,6},{5,7},{6,4},{7,5},{8,10},{9,11},{10,... | collective-permute-start | bytes 393224 | tf_op jit(solution)/shard_map/ppermute | solution.py:17
  86.5 24.0 %collective-permute-start.10 = (bf16[256,1024]{1,0:T(8,128)(2,1)S(1)}, bf16[256,1024]{1,0:T(8,128)(2,1)S(1)}, u32[]{:S(2)}, u32[]{:S(2)}) collective-permute-start(bf16[256,1024]{1,0:T(8,128)(2,1)S(1)} %shard_map.63.line_ref.refs_0_), channel_id=1, source_target_pairs={{0,1},{1,0},{2,3},{3,2},{4,5},{5,4},{6,7},{7,6},{8,9},{9,8},{10,11... | collective-permute-start | bytes 1572872 | tf_op jit(solution)/shard_map/ppermute | solution.py:17
  89.2 12.8 %collective-permute-start = (bf16[64,1024]{1,0:T(8,128)(2,1)S(1)}, bf16[64,1024]{1,0:T(8,128)(2,1)S(1)}, u32[]{:S(2)}, u32[]{:S(2)}) collective-permute-start(bf16[64,1024]{1,0:T(8,128)(2,1)S(1)} %get-tuple-element.36), channel_id=1, source_target_pairs={{0,2},{1,3},{2,0},{3,1},{4,6},{5,7},{6,4},{7,5},{8,10},{9,11},{10,... | collective-permute-start | bytes 393224 | tf_op jit(solution)/shard_map/ppermute | solution.py:17
  93.1 15.0 %collective-permute-start.1 = (bf16[64,1024]{1,0:T(8,128)(2,1)S(1)}, bf16[64,1024]{1,0:T(8,128)(2,1)S(1)}, u32[]{:S(2)}, u32[]{:S(2)}) collective-permute-start(bf16[64,1024]{1,0:T(8,128)(2,1)S(1)} %get-tuple-element.37), channel_id=1, source_target_pairs={{0,4},{1,5},{2,6},{3,7},{4,0},{5,1},{6,2},{7,3},{8,12},{9,13},{10,... | collective-permute-start | bytes 393224 | tf_op jit(solution)/shard_map/ppermute | solution.py:17
  97.1 12.0 %collective-permute-start.2 = (bf16[64,1024]{1,0:T(8,128)(2,1)S(1)}, bf16[64,1024]{1,0:T(8,128)(2,1)S(1)}, u32[]{:S(2)}, u32[]{:S(2)}) collective-permute-start(bf16[64,1024]{1,0:T(8,128)(2,1)S(1)} %get-tuple-element.38), channel_id=1, source_target_pairs={{0,6},{1,7},{2,4},{3,5},{4,2},{5,3},{6,0},{7,1},{8,14},{9,15},{10,... | collective-permute-start | bytes 393224 | tf_op jit(solution)/shard_map/ppermute | solution.py:17
  101.4 9.9 %collective-permute-start.17 = (bf16[64,1024]{1,0:T(8,128)(2,1)S(1)}, bf16[64,1024]{1,0:T(8,128)(2,1)S(1)}, u32[]{:S(2)}, u32[]{:S(2)}) collective-permute-start(bf16[64,1024]{1,0:T(8,128)(2,1)S(1)} %get-tuple-element.54), channel_id=1, source_target_pairs={{0,2},{1,3},{2,0},{3,1},{4,6},{5,7},{6,4},{7,5},{8,10},{9,11},{10,... | collective-permute-start | bytes 393224 | tf_op jit(solution)/shard_map/ppermute | solution.py:17
  102.0 15.6 %collective-permute-start.18 = (bf16[64,1024]{1,0:T(8,128)(2,1)S(1)}, bf16[64,1024]{1,0:T(8,128)(2,1)S(1)}, u32[]{:S(2)}, u32[]{:S(2)}) collective-permute-start(bf16[64,1024]{1,0:T(8,128)(2,1)S(1)} %get-tuple-element.55), channel_id=1, source_target_pairs={{0,4},{1,5},{2,6},{3,7},{4,0},{5,1},{6,2},{7,3},{8,12},{9,13},{10,... | collective-permute-start | bytes 393224 | tf_op jit(solution)/shard_map/ppermute | solution.py:17
  108.1 9.5 %collective-permute-start.19 = (bf16[64,1024]{1,0:T(8,128)(2,1)S(1)}, bf16[64,1024]{1,0:T(8,128)(2,1)S(1)}, u32[]{:S(2)}, u32[]{:S(2)}) collective-permute-start(bf16[64,1024]{1,0:T(8,128)(2,1)S(1)} %get-tuple-element.56), channel_id=1, source_target_pairs={{0,6},{1,7},{2,4},{3,5},{4,2},{5,3},{6,0},{7,1},{8,14},{9,15},{10,... | collective-permute-start | bytes 393224 | tf_op jit(solution)/shard_map/ppermute | solution.py:17
  109.8 14.8 %collective-permute-start.3 = (bf16[256,512]{1,0:T(8,128)(2,1)S(1)}, bf16[256,512]{1,0:T(8,128)(2,1)S(1)}, u32[]{:S(2)}, u32[]{:S(2)}) collective-permute-start(bf16[256,512]{1,0:T(8,128)(2,1)S(1)} %get-tuple-element.40), channel_id=1, source_target_pairs={{0,1},{1,0},{2,3},{3,2},{4,5},{5,4},{6,7},{7,6},{8,9},{9,8},{10,11... | collective-permute-start | bytes 786440 | tf_op jit(solution)/shard_map/ppermute | solution.py:17
  117.8 9.1 %collective-permute-start.26 = (bf16[64,1024]{1,0:T(8,128)(2,1)S(1)}, bf16[64,1024]{1,0:T(8,128)(2,1)S(1)}, u32[]{:S(2)}, u32[]{:S(2)}) collective-permute-start(bf16[64,1024]{1,0:T(8,128)(2,1)S(1)} %shard_map.68.refs_0_), channel_id=1, source_target_pairs={{0,7},{1,6},{2,5},{3,4},{4,3},{5,2},{6,1},{7,0},{8,15},{9,14},{10,... | collective-permute-start | bytes 393224 | tf_op jit(solution)/shard_map/ppermute | solution.py:17
  118.0 20.6 %collective-permute-start.25 = (bf16[64,1024]{1,0:T(8,128)(2,1)S(1)}, bf16[64,1024]{1,0:T(8,128)(2,1)S(1)}, u32[]{:S(2)}, u32[]{:S(2)}) collective-permute-start(bf16[64,1024]{1,0:T(8,128)(2,1)S(1)} %shard_map.68.refs_0_), channel_id=1, source_target_pairs={{0,5},{1,4},{2,7},{3,6},{4,1},{5,0},{6,3},{7,2},{8,13},{9,12},{10,... | collective-permute-start | bytes 393224 | tf_op jit(solution)/shard_map/ppermute | solution.py:17
  123.2 15.6 %collective-permute-start.24 = (bf16[64,1024]{1,0:T(8,128)(2,1)S(1)}, bf16[64,1024]{1,0:T(8,128)(2,1)S(1)}, u32[]{:S(2)}, u32[]{:S(2)}) collective-permute-start(bf16[64,1024]{1,0:T(8,128)(2,1)S(1)} %shard_map.68.refs_0_), channel_id=1, source_target_pairs={{0,3},{1,2},{2,1},{3,0},{4,7},{5,6},{6,5},{7,4},{8,11},{9,10},{10,... | collective-permute-start | bytes 393224 | tf_op jit(solution)/shard_map/ppermute | solution.py:17
  123.2 15.6 %collective-permute-start.23 = (bf16[64,1024]{1,0:T(8,128)(2,1)S(1)}, bf16[64,1024]{1,0:T(8,128)(2,1)S(1)}, u32[]{:S(2)}, u32[]{:S(2)}) collective-permute-start(bf16[64,1024]{1,0:T(8,128)(2,1)S(1)} %shard_map.68.refs_0_), channel_id=1, source_target_pairs={{0,1},{1,0},{2,3},{3,2},{4,5},{5,4},{6,7},{7,6},{8,9},{9,8},{10,11... | collective-permute-start | bytes 393224 | tf_op jit(solution)/shard_map/ppermute | solution.py:17
  124.6 14.2 %collective-permute-start.22 = (bf16[64,1024]{1,0:T(8,128)(2,1)S(1)}, bf16[64,1024]{1,0:T(8,128)(2,1)S(1)}, u32[]{:S(2)}, u32[]{:S(2)}) collective-permute-start(bf16[64,1024]{1,0:T(8,128)(2,1)S(1)} %shard_map.68.refs_0_), channel_id=1, source_target_pairs={{0,6},{1,7},{2,4},{3,5},{4,2},{5,3},{6,0},{7,1},{8,14},{9,15},{10,... | collective-permute-start | bytes 393224 | tf_op jit(solution)/shard_map/ppermute | solution.py:17
  126.9 11.9 %collective-permute-start.21 = (bf16[64,1024]{1,0:T(8,128)(2,1)S(1)}, bf16[64,1024]{1,0:T(8,128)(2,1)S(1)}, u32[]{:S(2)}, u32[]{:S(2)}) collective-permute-start(bf16[64,1024]{1,0:T(8,128)(2,1)S(1)} %shard_map.68.refs_0_), channel_id=1, source_target_pairs={{0,4},{1,5},{2,6},{3,7},{4,0},{5,1},{6,2},{7,3},{8,12},{9,13},{10,... | collective-permute-start | bytes 393224 | tf_op jit(solution)/shard_map/ppermute | solution.py:17
  138.6 5.0 %collective-permute-start.20 = (bf16[64,1024]{1,0:T(8,128)(2,1)S(1)}, bf16[64,1024]{1,0:T(8,128)(2,1)S(1)}, u32[]{:S(2)}, u32[]{:S(2)}) collective-permute-start(bf16[64,1024]{1,0:T(8,128)(2,1)S(1)} %shard_map.68.refs_0_), channel_id=1, source_target_pairs={{0,2},{1,3},{2,0},{3,1},{4,6},{5,7},{6,4},{7,5},{8,10},{9,11},{10,... | collective-permute-start | bytes 393224 | tf_op jit(solution)/shard_map/ppermute | solution.py:17
  144.6 2.0 %collective-permute-start.28 = (f32[128,1024]{1,0:T(8,128)S(1)}, f32[128,1024]{1,0:T(8,128)S(1)}, u32[]{:S(2)}, u32[]{:S(2)}) collective-permute-start(f32[128,1024]{1,0:T(8,128)S(1)} %get-tuple-element.60), channel_id=1, source_target_pairs={{0,8},{8,0},{16,24},{24,16},{1,9},{9,1},{17,25},{25,17},{2,10},{10... | collective-permute-start | bytes 1572872 | tf_op jit(solution)/shard_map/ppermute | solution.py:17
  145.7 2.1 %collective-permute-start.27 = (f32[128,1024]{1,0:T(8,128)S(1)}, f32[128,1024]{1,0:T(8,128)S(1)}, u32[]{:S(2)}, u32[]{:S(2)}) collective-permute-start(f32[128,1024]{1,0:T(8,128)S(1)} %get-tuple-element.58), channel_id=1, source_target_pairs={{0,8},{8,0},{16,24},{24,16},{1,9},{9,1},{17,25},{25,17},{2,10},{10... | collective-permute-start | bytes 1572872 | tf_op jit(solution)/shard_map/ppermute | solution.py:17
  146.6 8.4 %collective-permute-start.29 = (bf16[128,1024]{1,0:T(8,128)(2,1)S(1)}, bf16[128,1024]{1,0:T(8,128)(2,1)S(1)}, u32[]{:S(2)}, u32[]{:S(2)}) collective-permute-start(bf16[128,1024]{1,0:T(8,128)(2,1)S(1)} %shard_map.71), channel_id=1, source_target_pairs={{0,16},{8,24},{16,0},{24,8},{1,17},{9,25},{17,1},{25,9},{2,18},{10... | collective-permute-start | bytes 786440 | tf_op jit(solution)/shard_map/ppermute | solution.py:17

commit v2 on v1

--- a/solution.py
+++ b/solution.py
@@ -17,16 +17,19 @@
     return lax.ppermute(value, axis, [(i, i ^ mask) for i in range(count)])
 
 
-def call(body, scalars, arrays, outs, flops, scratch=(), to_hbm=False, from_hbm=False):
-    space = pltpu.HBM if from_hbm else pltpu.VMEM
-    arrays = [pltpu.with_memory_space_constraint(a, space) for a in arrays]
+def call(body, scalars, arrays, outs, flops, scratch=(), to_hbm=False, from_hbm=0):
+    far_away = [i >= len(arrays) - from_hbm for i in range(len(arrays))]
+    arrays = [
+        pltpu.with_memory_space_constraint(a, pltpu.HBM if there else pltpu.VMEM)
+        for a, there in zip(arrays, far_away)
+    ]
     make = jax.ShapeDtypeStruct if to_hbm else pltpu.VMEM
     size = sum(a.size * a.dtype.itemsize for a in arrays)
     head = [] if scalars is None else [scalars]
     return pl.pallas_call(
         body,
-        in_specs=[SMEM] * len(head) + [HBM if from_hbm else VMEM] * len(arrays),
-        out_specs=[VMEM] * len(outs),
+        in_specs=[SMEM] * len(head) + [HBM if there else VMEM for there in far_away],
+        out_specs=[HBM if to_hbm else VMEM] * len(outs),
         out_shape=[make(dims, dtype) for dims, dtype in outs],
         scratch_shapes=list(scratch),
         compiler_params=pltpu.CompilerParams(vmem_limit_bytes=24 << 20),
@@ -34,49 +37,66 @@
     )(*head, *arrays)
 
 
-def modulate(place, latents, shift, scale_mod):
+def modulate(place, latents, shift, scale_mod, bank):
     samples, depth = latents.shape
     rows = 16
     quarter = depth // 4
     steps = samples // rows
-
-    def body(place, x_hbm, b_hbm, s_hbm, hid_ref, lent_ref, own_ref, x_ref, b_ref, s_ref, sems):
+    forward, direct = shares(bank.shape[0])
+
+    def body(place, *refs):
+        sources, bank_hbm = refs[:3], refs[3]
+        hid_ref, lent_ref, own_ref, f_ref, d_ref = refs[4:9]
+        held, sems, row_sems = refs[9:12], refs[12], refs[13]
         side, core = place[0], place[1]
         copies = [
             [
                 pltpu.make_async_copy(src.at[pl.ds(r * rows, rows)], dst.at[r], sems.at[i, r])
-                for i, (src, dst) in enumerate(
-                    ((x_hbm, x_ref), (b_hbm, b_ref), (s_hbm, s_ref))
-                )
+                for i, (src, dst) in enumerate(zip(sources, held))
             ]
             for r in range(steps)
         ]
-        for group in copies:
+        starts = (2 * side + core) * forward, 4 * forward + core * direct
+        sent = [
+            pltpu.make_async_copy(
+                bank_hbm.at[pl.ds(pl.multiple_of(start, 16), ref.shape[0])], ref, row_sems.at[i]
+            )
+            for i, (start, ref) in enumerate(zip(starts, (f_ref, d_ref)))
+        ]
+        for group in copies + [sent]:
             for copy in group:
                 copy.start()
         for r in range(steps):
             for copy in copies[r]:
                 copy.wait()
             at = slice(r * rows, (r + 1) * rows)
-            x = x_ref[r].astype(F32)
+            x, b, s = (ref[r].astype(F32) for ref in held)
             inverse = lax.rsqrt(jnp.mean(x * x, axis=1, keepdims=True) + 1e-06)
-            hid_ref[at] = (
-                x * inverse * (1.0 + s_ref[r].astype(F32)) + b_ref[r].astype(F32)
-            ).astype(BF16)
+            hid_ref[at] = (x * inverse * (1.0 + s) + b).astype(BF16)
         for ref, s in ((lent_ref, 1 - side), (own_ref, side)):
             for i, c in enumerate((core, 1 - core)):
                 start = pl.multiple_of((2 * s + c) * quarter, quarter)
                 ref[:, i * quarter : (i + 1) * quarter] = hid_ref[:, pl.ds(start, quarter)]
+        for copy in sent:
+            copy.wait()
 
     half = (samples, depth // 2)
+    width = bank.shape[1]
     return call(
         body,
         place,
-        [latents, shift, scale_mod],
-        [((samples, depth), BF16), (half, BF16), (half, BF16)],
+        [latents, shift, scale_mod, bank],
+        [
+            ((samples, depth), BF16),
+            (half, BF16),
+            (half, BF16),
+            ((forward, width), BF16),
+            ((direct, width), BF16),
+        ],
         8 * samples * depth,
-        [pltpu.VMEM((steps, rows, depth), BF16)] * 3 + [pltpu.SemaphoreType.DMA((3, steps))],
-        from_hbm=True,
+        [pltpu.VMEM((steps, rows, depth), BF16)] * 3
+        + [pltpu.SemaphoreType.DMA((3, steps)), pltpu.SemaphoreType.DMA((2,))],
+        from_hbm=4,
     )
 
 
@@ -114,48 +134,79 @@
 
 
 def shares(rows):
-    return 9 * rows // 64, 14 * rows // 64
-
-
-def prepare(place, bank, weight):
+    return 19 * rows // 128, 26 * rows // 128
+
+
+def unit_rows(x):
+    x = x.astype(F32)
+    return (x / jnp.sqrt(jnp.sum(x * x, axis=1, keepdims=True) + 1e-06)).astype(BF16)
+
+
+def normalize_sent(forward, direct):
+    def body(a_ref, b_ref, f_ref, d_ref):
+        f_ref[...] = unit_rows(a_ref[...])
+        d_ref[...] = unit_rows(b_ref[...])
+
+    return call(
+        body,
+        None,
+        [forward, direct],
+        [(forward.shape, BF16), (direct.shape, BF16)],
+        8 * (forward.size + direct.size),
+    )
+
+
+def stage(place, hidden, weight, n_bank):
+    samples, depth = hidden.shape
+    pair = depth // 4 // n_bank * 2
+    count = n_bank // 2 if pair % 256 == 0 else 0
+
+    def body(place, hid_ref, w_hbm, o_ref, *refs):
+        copy = pltpu.make_async_copy(w_hbm, o_ref, refs[-1])
+        copy.start()
+        for i, ref in enumerate(refs[:-1]):
+            for g in range(4):
+                start = pl.multiple_of(g * (depth // 4) + (place[2] ^ i) * pair, pair)
+                ref[:, g * pair : (g + 1) * pair] = hid_ref[:, pl.ds(start, pair)]
+        copy.wait()
+
+    weight, *pieces = call(
+        body,
+        place,
+        [hidden, weight],
+        [(weight.shape, BF16)] + [((samples, 4 * pair), BF16)] * count,
+        0,
+        [pltpu.SemaphoreType.DMA(())],
+        from_hbm=1,
+    )
+    return weight, pieces
+
+
+def normalize(bank):
     rows, width = bank.shape
     steps = 8
     tile = rows // steps
-    forward, direct = shares(rows)
-
-    def body(place, x_hbm, w_hbm, o_ref, f_ref, d_ref, w_ref, x_ref, sems):
+
+    def body(x_hbm, o_ref, x_ref, sems):
         copies = [
             pltpu.make_async_copy(x_hbm.at[pl.ds(i * tile, tile)], x_ref.at[i], sems.at[i])
             for i in range(steps)
-        ] + [pltpu.make_async_copy(w_hbm, w_ref, sems.at[steps])]
+        ]
         for copy in copies:
             copy.start()
         for i in range(steps):
             copies[i].wait()
-            x = x_ref[i].astype(F32)
-            o_ref[i * tile : (i + 1) * tile] = (
-                x / jnp.sqrt(jnp.sum(x * x, axis=1, keepdims=True) + 1e-06)
-            ).astype(BF16)
-        start = pl.multiple_of((2 * place[0] + place[1]) * forward, 16)
-        f_ref[...] = o_ref[pl.ds(start, forward), :]
-        start = pl.multiple_of(4 * forward + place[1] * direct, 16)
-        d_ref[...] = o_ref[pl.ds(start, direct), :]
-        copies[steps].wait()
-
-    return call(
-        body,
-        place,
-        [bank, weight],
-        [
-            (bank.shape, BF16),
-            ((forward, width), BF16),
-            ((direct, width), BF16),
-            (weight.shape, BF16),
-        ],
+            o_ref[i * tile : (i + 1) * tile] = unit_rows(x_ref[i])
+
+    return call(
+        body,
+        None,
+        [bank],
+        [(bank.shape, BF16)],
         8 * bank.size,
-        [pltpu.VMEM((steps, tile, width), BF16), pltpu.SemaphoreType.DMA((steps + 1,))],
-        from_hbm=True,
-    )
+        [pltpu.VMEM((steps, tile, width), BF16), pltpu.SemaphoreType.DMA((steps,))],
+        from_hbm=1,
+    )[0]
 
 
 def join(pieces):
@@ -255,19 +306,6 @@
     )[0]
 
 
-def spread(place, hidden, n_bank):
-    samples, depth = hidden.shape
-    pair = depth // 4 // n_bank * 2
-
-    def body(place, hid_ref, *outs):
-        for i, ref in enumerate(outs):
-            for g in range(4):
-                start = pl.multiple_of(g * (depth // 4) + (place[2] ^ i) * pair, pair)
-                ref[:, g * pair : (g + 1) * pair] = hid_ref[:, pl.ds(start, pair)]
-
-    return call(body, place, [hidden], [((samples, 4 * pair), BF16)] * (n_bank // 2), 0)
-
-
 def split_pairs(place, pieces):
     samples, width = pieces[0].shape
     block = width // 8
@@ -296,19 +334,22 @@
     return call(body, None, [kept, given], [((width, 2 * rows), BF16)], 0)[0]
 
 
-def feature_sums(place, columns, grads, away):
+def feature_sums(place, columns, grads, blocks):
     samples, width = grads[0].shape
     count = len(grads)
     piece = columns.shape[0] // 4
+    batch = columns.shape[1]
+    fresh = count > 1
 
     def body(place, cols_ref, *refs):
-        ins, outs, held = refs[:count], refs[count : count + 2], refs[-1]
-        side, core = place[0], place[1]
-        for i in range(count):
-            held[i * samples : (i + 1) * samples] = ins[i][...]
-        s = 1 - side if away else side
-        for ref, c in zip(outs, (1 - core, core)):
-            start = pl.multiple_of((2 * s + c) * piece, piece)
+        ins, outs = refs[:count], refs[count:]
+        held = outs[-1] if fresh else ins[0]
+        if fresh:
+            for i in range(count):
+                held[i * samples : (i + 1) * samples] = ins[i][...]
+        for ref, (side, core) in zip(outs, blocks):
+            start = 2 * (place[0] ^ side) + (place[1] ^ core)
+            start = pl.multiple_of(start * piece, piece)
             ref[...] = jnp.dot(
                 cols_ref[pl.ds(start, piece), :], held[...], preferred_element_type=F32
             )
@@ -317,9 +358,8 @@
         body,
         place,
         [columns] + list(grads),
-        [((piece, width), F32)] * 2,
-        4 * piece * width * count * samples,
-        [pltpu.VMEM((count * samples, width), BF16)],
+        [((piece, width), F32)] * len(blocks) + [((batch, width), BF16)] * fresh,
+        2 * len(blocks) * piece * width * batch,
     )
 
 
@@ -340,32 +380,52 @@
         tile = squares[:, :128]
         for i in range(1, width // 128):
             tile = tile + squares[:, i * 128 : (i + 1) * 128]
+        tile = jnp.sum(tile, axis=0, keepdims=True)
         out_ref[...] = jnp.broadcast_to(tile[None], out_ref.shape)
 
     return call(
         body,
         None,
         [kept, from_core, from_side],
-        [((rows, width), F32), ((devices, 8, 128), F32)],
+        [((rows, width), F32), ((devices, 1, 128), F32)],
         4 * rows * width,
     )
 
 
 def scaled(gradient, squares, entries):
-    def body(g_ref, s_ref, o_ref):
+    rows = gradient.shape[0]
+    steps = 4 if rows % 32 == 0 else 1
+    size = rows // steps
+
+    def body(g_ref, s_ref, o_hbm, held, sems):
         mean = jnp.sum(s_ref[...]) / entries
-        o_ref[...] = g_ref[...] * lax.rsqrt(jnp.full((1, 1), mean + 1e-06, F32))
-
-    return call(
-        body, None, [gradient, squares], [(gradient.shape, F32)], gradient.size, (), True
+        factor = lax.rsqrt(jnp.full((1, 1), mean + 1e-06, F32))
+        copies = []
+        for i in range(steps):
+            at = slice(i * size, (i + 1) * size)
+            held[at] = g_ref[at] * factor
+            copies.append(
+                pltpu.make_async_copy(held.at[at], o_hbm.at[pl.ds(i * size, size)], sems.at[i])
+            )
+            copies[-1].start()
+        for copy in copies:
+            copy.wait()
+
+    return call(
+        body,
+        None,
+        [gradient, squares],
+        [(gradient.shape, F32)],
+        gradient.size,
+        [pltpu.VMEM(gradient.shape, F32), pltpu.SemaphoreType.DMA((steps,))],
+        to_hbm=True,
     )[0]
 
 
-def by_feature(place, hidden, n_bank):
+def by_feature(place, hidden, pieces, n_bank):
     samples, depth = hidden.shape
     piece = depth // 4 // n_bank
-    if piece % 128 == 0:
-        pieces = spread(place, hidden, n_bank)
+    if pieces:
         pieces = [swap(p, "bank", 2 * i) if i else p for i, p in enumerate(pieces)]
         kept, given = split_pairs(place, pieces)
         return turn(kept, swap(given, "bank", 1))
@@ -392,43 +452,45 @@
     evens, odds = list(range(0, n_bank, 2)), list(range(1, n_bank, 2))
 
     head_other = swap(head_weight, "gen", 1)
-    hidden, lent, own = modulate(place, latents, shift, scale_mod)
-    bank, head_weight, lent = lax.optimization_barrier((bank, head_weight, lent))
+    hidden, lent, own, forward, direct = modulate(place, latents, shift, scale_mod, bank)
     lent = swap(lent, "gen", 2)
-    bank_unit, forward, direct, head_weight = prepare(place, bank, head_weight)
+    forward, direct = normalize_sent(forward, direct)
+    head_weight, pieces = stage(place, hidden, head_weight, n_bank)
+    bank_unit = normalize(bank)
     own_part = project(own, head_weight, head_other)
     returned = swap(project(lent, head_weight, head_other), "gen", 2)
     exact, unit, length = finish_embed(own_part, returned)
 
-    columns = by_feature(place, hidden, n_bank)
+    columns = by_feature(place, hidden, pieces, n_bank)
 
     forward = swap(forward, "bank", 1)
     direct = swap(direct, "bank", 1)
     beside = swap(forward, "gen", 2)
     early = [forward, swap(forward, "gen", 1)]
-    late = [beside, direct]
-    late += [swap(v, "gen", 1) for v in late]
+    middle = [beside, direct]
+    late = [swap(v, "gen", 1) for v in middle]
 
     line = [unit] + [swap(unit, "bank", m) for m in evens[1:]]
     line = join(line)
     across = swap(line, "bank", 1)
-    sums = bank_sums(line, [bank_unit])[0]
-    sums = bank_sums(line, early, sums)[0]
+    sums = bank_sums(line, [bank_unit] + early)[0]
+    sums = bank_sums(line, middle, sums)[0]
     far = bank_sums(line, late, sums, samples)
     parts = [swap(v, "bank", m) for m, v in zip(evens[1:], far[1:])]
     near = pair_sums(unit, line, across)
     grad_embed = embed_gradient(near, far[0], parts, exact, length, bank.shape[0] * n_bank)
 
     grads = {0: grad_embed}
-    for m in range(n_bank - 1, 0, -1):
+    for m in range(n_bank - 2, 0, -1):
         grads[m] = swap(grad_embed, "bank", m)
+    grads[n_bank - 1] = swap(grads[n_bank - 2], "bank", 1)
     grads = [grads[m] for m in evens + odds]
-    for_core, ours = feature_sums(place, columns, grads, True)
-    away = add_round(ours, swap(for_core, "gen", 1))
-    for_core, ours = feature_sums(place, columns, grads, False)
-    gradient, squares = square_sums(
-        ours, swap(for_core, "gen", 1), swap(away, "gen", 2), n_gen * n_bank
-    )
+    for_core, grads = feature_sums(place, columns, grads, [(1, 1)])
+    for_core = swap(for_core, "gen", 1)
+    away, ours, home = feature_sums(place, columns, [grads], [(1, 0), (0, 0), (0, 1)])
+    away = swap(add_round(away, for_core), "gen", 2)
+    home = swap(home, "gen", 1)
+    gradient, squares = square_sums(ours, home, away, n_gen * n_bank)
     squares = lax.all_to_all(squares, ("gen", "bank"), 0, 0, tiled=True)
     return scaled(gradient, squares, depth * width)
 

time: 167 us -> 138 us (0.83)
  waiting for transfers between devices: 92.7 us -> 62.4 us
  Pallas kernels: 20.2 us -> 21.9 us
    ppermute x30, waiting for transfers between devices: 92.7 us -> 62.4 us  [swap(): return lax.ppermute(value, axis, [(i, i ^ mask) for i in range(count)])]
    pallas_call x19 -> x20, Pallas kernels: 20.2 us -> 21.9 us  [call(): pl.pallas_call(body, in_specs=[SMEM] * len(head) + [HBM if there else VME...]
  transfers between devices with their start and end apart: 30 -> 30, of which waited for: 14 -> 13; matrix products, arithmetic and copies ran while one was open for 0% -> 0% of each run, Pallas kernels for 11% -> 14%
where the time goes in v2:
time: 138 us
  waiting for transfers between devices  62.4 us (45%)
  starting transfers between devices  42.1 us (31%)
  Pallas kernels  21.9 us (16%)
  blocking collectives  11.2 us (8%)
    ppermute x30, waiting for transfers between devices, swap(): return lax.ppermute(value, axis, [(i, i ^ mask) for i in range(count)])  62.4 us
    ppermute x30, starting transfers between devices, swap(): return lax.ppermute(value, axis, [(i, i ^ mask) for i in range(count)])  42.1 us
    pallas_call x20, Pallas kernels, call(): pl.pallas_call(body, in_specs=[SMEM] * len(head) + [HBM if there else VME...  21.9 us
    all_to_all x1, blocking collectives, local(): squares = lax.all_to_all(squares, ('gen', 'bank'), 0, 0, tiled=True)  11.2 us
  transfers between devices with their start and end apart: 30, of which 13 were waited for; matrix products, arithmetic and copies ran while one was open for 0% of the time, Pallas kernels for 14%

profile of v2, /device:TPU:0, one launch (start us, length us, event | category | flops | bytes accessed | tf_op | source)
XLA Modules:
  0.0 137.8 jit_solution(16230592726667094200)
XLA Ops:
  0.6 2.6 %shard_map.55 = (bf16[64,4096]{1,0:T(8,128)(2,1)S(1)}, bf16[64,2048]{1,0:T(8,128)(2,1)S(1)}, bf16[64,2048]{1,0:T(8,128)(2,1)S(1)}, bf16[304,1024]{1,0:T(8,128)(2,1)S(1)}, bf16[416,1024]{1,0:T(8,128)(2,1)S(1)}) custom-call(s32[4]{0:T(128)S(1)} %pad_add_fusion.place, bf16[64,4096]{1,0:T(8,128)(2,1)} %refs_0_.1, bf16[64,4096]{1,0:T(8,128)(2,1)} %refs_1_.1, ...), custom_call_target="tpu_custom_call" | custom-call | flops 2097152 | bytes 5767168 | tf_op jit(solution)/shard_map/pallas_call | solution.py:29
  3.7 2.6 %collective-permute-start.11 = (bf16[304,1024]{1,0:T(8,128)(2,1)S(1)}, bf16[304,1024]{1,0:T(8,128)(2,1)S(1)}, u32[]{:S(2)}, u32[]{:S(2)}) collective-permute-start(bf16[304,1024]{1,0:T(8,128)(2,1)S(1)} %get-tuple-element.46), channel_id=1, source_target_pairs={{0,1},{1,0},{2,3},{3,2},{4,5},{5,4},{6,7},{7,6},{8,9},{9,8},{10,11... | collective-permute-start | bytes 1867784 | tf_op jit(solution)/shard_map/ppermute | solution.py:17
  6.4 14.8 %collective-permute-done.11.refs_2_ = bf16[304,1024]{1,0:T(8,128)(2,1)S(1)} collective-permute-done((bf16[304,1024]{1,0:T(8,128)(2,1)S(1)}, bf16[304,1024]{1,0:T(8,128)(2,1)S(1)}, u32[]{:S(2)}, u32[]{:S(2)}) %collective-permute-start.11) | collective-permute-done | bytes 622624 | tf_op jit(solution)/shard_map/ppermute | solution.py:17
  21.2 2.0 %collective-permute-start.12 = (bf16[304,1024]{1,0:T(8,128)(2,1)S(1)}, bf16[304,1024]{1,0:T(8,128)(2,1)S(1)}, u32[]{:S(2)}, u32[]{:S(2)}) collective-permute-start(bf16[304,1024]{1,0:T(8,128)(2,1)S(1)} %collective-permute-done.11.refs_2_), channel_id=1, source_target_pairs={{0,16},{8,24},{16,0},{24,8},{1,17},{9,25},{17,1},{25,9},{2,18},{10... | collective-permute-start | bytes 1867784 | tf_op jit(solution)/shard_map/ppermute | solution.py:17
  23.2 16.0 %collective-permute-done.14.refs_2_ = bf16[416,1024]{1,0:T(8,128)(2,1)S(1)} collective-permute-done((bf16[416,1024]{1,0:T(8,128)(2,1)S(1)}, bf16[416,1024]{1,0:T(8,128)(2,1)S(1)}, u32[]{:S(2)}, u32[]{:S(2)}) %collective-permute-start.14) | collective-permute-done | bytes 852000 | tf_op jit(solution)/shard_map/ppermute | solution.py:17
  39.3 2.1 %shard_map.56 = (bf16[1024,1024]{1,0:T(8,128)(2,1)S(1)}, bf16[64,1024]{1,0:T(8,128)(2,1)S(1)}, bf16[64,1024]{1,0:T(8,128)(2,1)S(1)}, bf16[64,1024]{1,0:T(8,128)(2,1)S(1)}, bf16[64,1024]{1,0:T(8,128)(2,1)S(1)}) custom-call(s32[4]{0:T(128)S(1)} %pad_add_fusion.place, bf16[64,4096]{1,0:T(8,128)(2,1)S(1)} %get-tuple-element.33.hid_ref, bf16[1024,1024]{1,0:T(8,128)(2,1)} %w_hbm.1), custom_call_target="tpu_custom_call" | custom-call | bytes 2621440 | tf_op jit(solution)/shard_map/pallas_call | solution.py:29
  43.3 1.5 %collective-permute-start.6 = (f32[64,1024]{1,0:T(8,128)S(1)}, f32[64,1024]{1,0:T(8,128)S(1)}, u32[]{:S(2)}, u32[]{:S(2)}) collective-permute-start(f32[64,1024]{1,0:T(8,128)S(1)} %shard_map.60), channel_id=1, source_target_pairs={{0,16},{8,24},{16,0},{24,8},{1,17},{9,25},{17,1},{25,9},{2,18},{10... | collective-permute-start | bytes 786440 | tf_op jit(solution)/shard_map/ppermute | solution.py:17
  45.7 5.4 %collective-permute-done.6.b_ref = f32[64,1024]{1,0:T(8,128)S(1)} collective-permute-done((f32[64,1024]{1,0:T(8,128)S(1)}, f32[64,1024]{1,0:T(8,128)S(1)}, u32[]{:S(2)}, u32[]{:S(2)}) %collective-permute-start.6) | collective-permute-done | bytes 262176 | tf_op jit(solution)/shard_map/ppermute | solution.py:17
  51.2 1.9 %collective-permute-start.7 = (bf16[64,1024]{1,0:T(8,128)(2,1)S(1)}, bf16[64,1024]{1,0:T(8,128)(2,1)S(1)}, u32[]{:S(2)}, u32[]{:S(2)}) collective-permute-start(bf16[64,1024]{1,0:T(8,128)(2,1)S(1)} %get-tuple-element.43.refs_0_.unit_ref), channel_id=1, source_target_pairs={{0,2},{1,3},{2,0},{3,1},{4,6},{5,7},{6,4},{7,5},{8,10},{9,11},{10,... | collective-permute-start | bytes 393224 | tf_op jit(solution)/shard_map/ppermute | solution.py:17
  53.1 2.6 %collective-permute-start.8 = (bf16[64,1024]{1,0:T(8,128)(2,1)S(1)}, bf16[64,1024]{1,0:T(8,128)(2,1)S(1)}, u32[]{:S(2)}, u32[]{:S(2)}) collective-permute-start(bf16[64,1024]{1,0:T(8,128)(2,1)S(1)} %get-tuple-element.43.refs_0_.unit_ref), channel_id=1, source_target_pairs={{0,4},{1,5},{2,6},{3,7},{4,0},{5,1},{6,2},{7,3},{8,12},{9,13},{10,... | collective-permute-start | bytes 393224 | tf_op jit(solution)/shard_map/ppermute | solution.py:17
  55.7 2.1 %collective-permute-done.7.refs_1_ = bf16[64,1024]{1,0:T(8,128)(2,1)S(1)} collective-permute-done((bf16[64,1024]{1,0:T(8,128)(2,1)S(1)}, bf16[64,1024]{1,0:T(8,128)(2,1)S(1)}, u32[]{:S(2)}, u32[]{:S(2)}) %collective-permute-start.7) | collective-permute-done | bytes 131104 | tf_op jit(solution)/shard_map/ppermute | solution.py:17
  57.8 3.6 %collective-permute-start.9 = (bf16[64,1024]{1,0:T(8,128)(2,1)S(1)}, bf16[64,1024]{1,0:T(8,128)(2,1)S(1)}, u32[]{:S(2)}, u32[]{:S(2)}) collective-permute-start(bf16[64,1024]{1,0:T(8,128)(2,1)S(1)} %get-tuple-element.43.refs_0_.unit_ref), channel_id=1, source_target_pairs={{0,6},{1,7},{2,4},{3,5},{4,2},{5,3},{6,0},{7,1},{8,14},{9,15},{10,... | collective-permute-start | bytes 393224 | tf_op jit(solution)/shard_map/ppermute | solution.py:17
  61.3 3.3 %collective-permute-done.8.refs_2_ = bf16[64,1024]{1,0:T(8,128)(2,1)S(1)} collective-permute-done((bf16[64,1024]{1,0:T(8,128)(2,1)S(1)}, bf16[64,1024]{1,0:T(8,128)(2,1)S(1)}, u32[]{:S(2)}, u32[]{:S(2)}) %collective-permute-start.8) | collective-permute-done | bytes 131104 | tf_op jit(solution)/shard_map/ppermute | solution.py:17
  64.7 2.0 %collective-permute-start.10 = (bf16[256,1024]{1,0:T(8,128)(2,1)S(1)}, bf16[256,1024]{1,0:T(8,128)(2,1)S(1)}, u32[]{:S(2)}, u32[]{:S(2)}) collective-permute-start(bf16[256,1024]{1,0:T(8,128)(2,1)S(1)} %shard_map.62.line_ref.refs_0_), channel_id=1, source_target_pairs={{0,1},{1,0},{2,3},{3,2},{4,5},{5,4},{6,7},{7,6},{8,9},{9,8},{10,11... | collective-permute-start | bytes 1572872 | tf_op jit(solution)/shard_map/ppermute | solution.py:17
  66.7 1.9 %collective-permute-start = (bf16[64,1024]{1,0:T(8,128)(2,1)S(1)}, bf16[64,1024]{1,0:T(8,128)(2,1)S(1)}, u32[]{:S(2)}, u32[]{:S(2)}) collective-permute-start(bf16[64,1024]{1,0:T(8,128)(2,1)S(1)} %get-tuple-element.35), channel_id=1, source_target_pairs={{0,2},{1,3},{2,0},{3,1},{4,6},{5,7},{6,4},{7,5},{8,10},{9,11},{10,... | collective-permute-start | bytes 393224 | tf_op jit(solution)/shard_map/ppermute | solution.py:17
  68.6 2.8 %shard_map.65.refs_1_ = bf16[2048,1024]{1,0:T(8,128)(2,1)S(1)} custom-call(bf16[2048,1024]{1,0:T(8,128)(2,1)} %x_hbm.1), custom_call_target="tpu_custom_call" | custom-call | flops 16777216 | bytes 4194304 | tf_op jit(solution)/shard_map/pallas_call | solution.py:29
  71.5 1.8 %collective-permute-start.1 = (bf16[64,1024]{1,0:T(8,128)(2,1)S(1)}, bf16[64,1024]{1,0:T(8,128)(2,1)S(1)}, u32[]{:S(2)}, u32[]{:S(2)}) collective-permute-start(bf16[64,1024]{1,0:T(8,128)(2,1)S(1)} %get-tuple-element.36), channel_id=1, source_target_pairs={{0,4},{1,5},{2,6},{3,7},{4,0},{5,1},{6,2},{7,3},{8,12},{9,13},{10,... | collective-permute-start | bytes 393224 | tf_op jit(solution)/shard_map/ppermute | solution.py:17
  73.3 4.0 %shard_map.66.refs_3_ = f32[256,1024]{1,0:T(8,128)S(1)} custom-call(bf16[256,1024]{1,0:T(8,128)(2,1)S(1)} %shard_map.62.line_ref.refs_0_, bf16[2048,1024]{1,0:T(8,128)(2,1)S(1)} %shard_map.65.refs_1_, bf16[304,1024]{1,0:T(8,128)(2,1)S(1)} %collective-permute-done.11.refs_2_, bf16[304,1024]{1,0:T(8,128)(2,1)S(1)} %collective-permute-done.16.refs_3_), custom_call_target="tpu_custom_call" | custom-call | flops 2785017856 | bytes 5963776 | tf_op jit(solution)/shard_map/pallas_call | solution.py:29
  78.3 1.5 %shard_map.67.refs_3_ = f32[256,1024]{1,0:T(8,128)S(1)} custom-call(bf16[256,1024]{1,0:T(8,128)(2,1)S(1)} %shard_map.62.line_ref.refs_0_, bf16[304,1024]{1,0:T(8,128)(2,1)S(1)} %collective-permute-done.12.refs_1_, bf16[416,1024]{1,0:T(8,128)(2,1)S(1)} %collective-permute-done.14.refs_2_, f32[256,1024]{1,0:T(8,128)S(1)} %shard_map.66.refs_3_), custom_call_target="tpu_custom_call" | custom-call | flops 754974720 | bytes 3047424 | tf_op jit(solution)/shard_map/pallas_call | solution.py:29
  79.8 1.5 %shard_map.68 = (f32[64,1024]{1,0:T(8,128)S(1)}, bf16[64,1024]{1,0:T(8,128)(2,1)S(1)}, bf16[64,1024]{1,0:T(8,128)(2,1)S(1)}, bf16[64,1024]{1,0:T(8,128)(2,1)S(1)}) custom-call(bf16[256,1024]{1,0:T(8,128)(2,1)S(1)} %shard_map.62.line_ref.refs_0_, bf16[304,1024]{1,0:T(8,128)(2,1)S(1)} %collective-permute-done.13.refs_1_, ...), custom_call_target="tpu_custom_call" | custom-call | flops 754974720 | bytes 3047424 | tf_op jit(solution)/shard_map/pallas_call | solution.py:29
  82.2 2.6 %collective-permute-start.18 = (bf16[64,1024]{1,0:T(8,128)(2,1)S(1)}, bf16[64,1024]{1,0:T(8,128)(2,1)S(1)}, u32[]{:S(2)}, u32[]{:S(2)}) collective-permute-start(bf16[64,1024]{1,0:T(8,128)(2,1)S(1)} %get-tuple-element.52), channel_id=1, source_target_pairs={{0,4},{1,5},{2,6},{3,7},{4,0},{5,1},{6,2},{7,3},{8,12},{9,13},{10,... | collective-permute-start | bytes 393224 | tf_op jit(solution)/shard_map/ppermute | solution.py:17
  87.8 1.8 %collective-permute-done.17.refs_4_ = bf16[64,1024]{1,0:T(8,128)(2,1)S(1)} collective-permute-done((bf16[64,1024]{1,0:T(8,128)(2,1)S(1)}, bf16[64,1024]{1,0:T(8,128)(2,1)S(1)}, u32[]{:S(2)}, u32[]{:S(2)}) %collective-permute-start.17) | collective-permute-done | bytes 131104 | tf_op jit(solution)/shard_map/ppermute | solution.py:17
  89.6 4.5 %collective-permute-done.18.refs_5_ = bf16[64,1024]{1,0:T(8,128)(2,1)S(1)} collective-permute-done((bf16[64,1024]{1,0:T(8,128)(2,1)S(1)}, bf16[64,1024]{1,0:T(8,128)(2,1)S(1)}, u32[]{:S(2)}, u32[]{:S(2)}) %collective-permute-start.18) | collective-permute-done | bytes 131104 | tf_op jit(solution)/shard_map/ppermute | solution.py:17
  94.3 2.9 %collective-permute-start.22 = (bf16[64,1024]{1,0:T(8,128)(2,1)S(1)}, bf16[64,1024]{1,0:T(8,128)(2,1)S(1)}, u32[]{:S(2)}, u32[]{:S(2)}) collective-permute-start(bf16[64,1024]{1,0:T(8,128)(2,1)S(1)} %shard_map.69.refs_0_), channel_id=1, source_target_pairs={{0,6},{1,7},{2,4},{3,5},{4,2},{5,3},{6,0},{7,1},{8,14},{9,15},{10,... | collective-permute-start | bytes 393224 | tf_op jit(solution)/shard_map/ppermute | solution.py:17
  99.3 2.7 %collective-permute-start.24 = (bf16[64,1024]{1,0:T(8,128)(2,1)S(1)}, bf16[64,1024]{1,0:T(8,128)(2,1)S(1)}, u32[]{:S(2)}, u32[]{:S(2)}) collective-permute-start(bf16[64,1024]{1,0:T(8,128)(2,1)S(1)} %shard_map.69.refs_0_), channel_id=1, source_target_pairs={{0,3},{1,2},{2,1},{3,0},{4,7},{5,6},{6,5},{7,4},{8,11},{9,10},{10,... | collective-permute-start | bytes 393224 | tf_op jit(solution)/shard_map/ppermute | solution.py:17
  102.6 4.4 %collective-permute-start.25 = (bf16[64,1024]{1,0:T(8,128)(2,1)S(1)}, bf16[64,1024]{1,0:T(8,128)(2,1)S(1)}, u32[]{:S(2)}, u32[]{:S(2)}) collective-permute-start(bf16[64,1024]{1,0:T(8,128)(2,1)S(1)} %shard_map.69.refs_0_), channel_id=1, source_target_pairs={{0,5},{1,4},{2,7},{3,6},{4,1},{5,0},{6,3},{7,2},{8,13},{9,12},{10,... | collective-permute-start | bytes 393224 | tf_op jit(solution)/shard_map/ppermute | solution.py:17
  107.0 1.5 %collective-permute-start.26 = (bf16[64,1024]{1,0:T(8,128)(2,1)S(1)}, bf16[64,1024]{1,0:T(8,128)(2,1)S(1)}, u32[]{:S(2)}, u32[]{:S(2)}) collective-permute-start(bf16[64,1024]{1,0:T(8,128)(2,1)S(1)} %collective-permute-done.22.refs_3_), channel_id=1, source_target_pairs={{0,1},{1,0},{2,3},{3,2},{4,5},{5,4},{6,7},{7,6},{8,9},{9,8},{10,11... | collective-permute-start | bytes 393224 | tf_op jit(solution)/shard_map/ppermute | solution.py:17
  108.7 3.7 %collective-permute-done.21.refs_2_ = bf16[64,1024]{1,0:T(8,128)(2,1)S(1)} collective-permute-done((bf16[64,1024]{1,0:T(8,128)(2,1)S(1)}, bf16[64,1024]{1,0:T(8,128)(2,1)S(1)}, u32[]{:S(2)}, u32[]{:S(2)}) %collective-permute-start.21) | collective-permute-done | bytes 131104 | tf_op jit(solution)/shard_map/ppermute | solution.py:17
  112.5 1.7 %collective-permute-done.25.refs_6_ = bf16[64,1024]{1,0:T(8,128)(2,1)S(1)} collective-permute-done((bf16[64,1024]{1,0:T(8,128)(2,1)S(1)}, bf16[64,1024]{1,0:T(8,128)(2,1)S(1)}, u32[]{:S(2)}, u32[]{:S(2)}) %collective-permute-start.25) | collective-permute-done | bytes 131104 | tf_op jit(solution)/shard_map/ppermute | solution.py:17
  117.1 1.4 %collective-permute-start.29 = (bf16[128,1024]{1,0:T(8,128)(2,1)S(1)}, bf16[128,1024]{1,0:T(8,128)(2,1)S(1)}, u32[]{:S(2)}, u32[]{:S(2)}) collective-permute-start(bf16[128,1024]{1,0:T(8,128)(2,1)S(1)} %shard_map.72), channel_id=1, source_target_pairs={{0,16},{8,24},{16,0},{24,8},{1,17},{9,25},{17,1},{25,9},{2,18},{10... | collective-permute-start | bytes 786440 | tf_op jit(solution)/shard_map/ppermute | solution.py:17
  118.5 7.0 %collective-permute-done.29.c_ref = bf16[128,1024]{1,0:T(8,128)(2,1)S(1)} collective-permute-done((bf16[128,1024]{1,0:T(8,128)(2,1)S(1)}, bf16[128,1024]{1,0:T(8,128)(2,1)S(1)}, u32[]{:S(2)}, u32[]{:S(2)}) %collective-permute-start.29) | collective-permute-done | bytes 262176 | tf_op jit(solution)/shard_map/ppermute | solution.py:17
  125.7 11.2 %all_to_all.5.s_ref = f32[32,1,128]{2,1,0:T(1,128)S(1)} all-to-all(f32[32,1,128]{2,1,0:T(1,128)S(1)} %get-tuple-element.60), channel_id=1, replica_groups=mesh['gen'=4,'bank'=8] {'gen','bank'}, dimensions={0} | all-to-all | bytes 32768 | tf_op jit(solution)/shard_map/all_to_all | solution.py:494
  (50 shorter events, 16.3 us)
Async XLA Ops:
  0.0 42.5 %collective-permute-start.4 = (bf16[1024,1024]{1,0:T(8,128)(2,1)}, bf16[1024,1024]{1,0:T(8,128)(2,1)S(1)}, u32[]{:S(2)}, u32[]{:S(2)}) collective-permute-start(bf16[1024,1024]{1,0:T(8,128)(2,1)} %w_hbm.1), channel_id=1, source_target_pairs={{0,8},{8,0},{16,24},{24,16},{1,9},{9,1},{17,25},{25,17},{2,10},{10... | collective-permute-start | bytes 6291464 | tf_op jit(solution)/shard_map/ppermute | solution.py:17
  3.7 17.5 %collective-permute-start.11 = (bf16[304,1024]{1,0:T(8,128)(2,1)S(1)}, bf16[304,1024]{1,0:T(8,128)(2,1)S(1)}, u32[]{:S(2)}, u32[]{:S(2)}) collective-permute-start(bf16[304,1024]{1,0:T(8,128)(2,1)S(1)} %get-tuple-element.46), channel_id=1, source_target_pairs={{0,1},{1,0},{2,3},{3,2},{4,5},{5,4},{6,7},{7,6},{8,9},{9,8},{10,11... | collective-permute-start | bytes 1867784 | tf_op jit(solution)/shard_map/ppermute | solution.py:17
  6.3 33.0 %collective-permute-start.14 = (bf16[416,1024]{1,0:T(8,128)(2,1)S(1)}, bf16[416,1024]{1,0:T(8,128)(2,1)S(1)}, u32[]{:S(2)}, u32[]{:S(2)}) collective-permute-start(bf16[416,1024]{1,0:T(8,128)(2,1)S(1)} %get-tuple-element.47), channel_id=1, source_target_pairs={{0,1},{1,0},{2,3},{3,2},{4,5},{5,4},{6,7},{7,6},{8,9},{9,8},{10,11... | collective-permute-start | bytes 2555912 | tf_op jit(solution)/shard_map/ppermute | solution.py:17
  21.2 23.7 %collective-permute-start.12 = (bf16[304,1024]{1,0:T(8,128)(2,1)S(1)}, bf16[304,1024]{1,0:T(8,128)(2,1)S(1)}, u32[]{:S(2)}, u32[]{:S(2)}) collective-permute-start(bf16[304,1024]{1,0:T(8,128)(2,1)S(1)} %collective-permute-done.11.refs_2_), channel_id=1, source_target_pairs={{0,16},{8,24},{16,0},{24,8},{1,17},{9,25},{17,1},{25,9},{2,18},{10... | collective-permute-start | bytes 1867784 | tf_op jit(solution)/shard_map/ppermute | solution.py:17
  23.2 19.3 %collective-permute-start.5 = (bf16[64,2048]{1,0:T(8,128)(2,1)S(1)}, bf16[64,2048]{1,0:T(8,128)(2,1)S(1)}, u32[]{:S(2)}, u32[]{:S(2)}) collective-permute-start(bf16[64,2048]{1,0:T(8,128)(2,1)S(1)} %get-tuple-element.42), channel_id=1, source_target_pairs={{0,16},{8,24},{16,0},{24,8},{1,17},{9,25},{17,1},{25,9},{2,18},{10... | collective-permute-start | bytes 786440 | tf_op jit(solution)/shard_map/ppermute | solution.py:17
  23.2 48.3 %collective-permute-start.16 = (bf16[304,1024]{1,0:T(8,128)(2,1)S(1)}, bf16[304,1024]{1,0:T(8,128)(2,1)S(1)}, u32[]{:S(2)}, u32[]{:S(2)}) collective-permute-start(bf16[304,1024]{1,0:T(8,128)(2,1)S(1)} %collective-permute-done.11.refs_2_), channel_id=1, source_target_pairs={{0,8},{8,0},{16,24},{24,16},{1,9},{9,1},{17,25},{25,17},{2,10},{10... | collective-permute-start | bytes 1867784 | tf_op jit(solution)/shard_map/ppermute | solution.py:17
  39.3 38.0 %collective-permute-start.15 = (bf16[416,1024]{1,0:T(8,128)(2,1)S(1)}, bf16[416,1024]{1,0:T(8,128)(2,1)S(1)}, u32[]{:S(2)}, u32[]{:S(2)}) collective-permute-start(bf16[416,1024]{1,0:T(8,128)(2,1)S(1)} %collective-permute-done.14.refs_2_), channel_id=1, source_target_pairs={{0,8},{8,0},{16,24},{24,16},{1,9},{9,1},{17,25},{25,17},{2,10},{10... | collective-permute-start | bytes 2555912 | tf_op jit(solution)/shard_map/ppermute | solution.py:17
  43.3 7.7 %collective-permute-start.6 = (f32[64,1024]{1,0:T(8,128)S(1)}, f32[64,1024]{1,0:T(8,128)S(1)}, u32[]{:S(2)}, u32[]{:S(2)}) collective-permute-start(f32[64,1024]{1,0:T(8,128)S(1)} %shard_map.60), channel_id=1, source_target_pairs={{0,16},{8,24},{16,0},{24,8},{1,17},{9,25},{17,1},{25,9},{2,18},{10... | collective-permute-start | bytes 786440 | tf_op jit(solution)/shard_map/ppermute | solution.py:17
  44.8 35.0 %collective-permute-start.13 = (bf16[304,1024]{1,0:T(8,128)(2,1)S(1)}, bf16[304,1024]{1,0:T(8,128)(2,1)S(1)}, u32[]{:S(2)}, u32[]{:S(2)}) collective-permute-start(bf16[304,1024]{1,0:T(8,128)(2,1)S(1)} %collective-permute-done.12.refs_1_), channel_id=1, source_target_pairs={{0,8},{8,0},{16,24},{24,16},{1,9},{9,1},{17,25},{25,17},{2,10},{10... | collective-permute-start | bytes 1867784 | tf_op jit(solution)/shard_map/ppermute | solution.py:17
  51.2 6.5 %collective-permute-start.7 = (bf16[64,1024]{1,0:T(8,128)(2,1)S(1)}, bf16[64,1024]{1,0:T(8,128)(2,1)S(1)}, u32[]{:S(2)}, u32[]{:S(2)}) collective-permute-start(bf16[64,1024]{1,0:T(8,128)(2,1)S(1)} %get-tuple-element.43.refs_0_.unit_ref), channel_id=1, source_target_pairs={{0,2},{1,3},{2,0},{3,1},{4,6},{5,7},{6,4},{7,5},{8,10},{9,11},{10,... | collective-permute-start | bytes 393224 | tf_op jit(solution)/shard_map/ppermute | solution.py:17
  53.1 11.6 %collective-permute-start.8 = (bf16[64,1024]{1,0:T(8,128)(2,1)S(1)}, bf16[64,1024]{1,0:T(8,128)(2,1)S(1)}, u32[]{:S(2)}, u32[]{:S(2)}) collective-permute-start(bf16[64,1024]{1,0:T(8,128)(2,1)S(1)} %get-tuple-element.43.refs_0_.unit_ref), channel_id=1, source_target_pairs={{0,4},{1,5},{2,6},{3,7},{4,0},{5,1},{6,2},{7,3},{8,12},{9,13},{10,... | collective-permute-start | bytes 393224 | tf_op jit(solution)/shard_map/ppermute | solution.py:17
  57.8 6.9 %collective-permute-start.9 = (bf16[64,1024]{1,0:T(8,128)(2,1)S(1)}, bf16[64,1024]{1,0:T(8,128)(2,1)S(1)}, u32[]{:S(2)}, u32[]{:S(2)}) collective-permute-start(bf16[64,1024]{1,0:T(8,128)(2,1)S(1)} %get-tuple-element.43.refs_0_.unit_ref), channel_id=1, source_target_pairs={{0,6},{1,7},{2,4},{3,5},{4,2},{5,3},{6,0},{7,1},{8,14},{9,15},{10,... | collective-permute-start | bytes 393224 | tf_op jit(solution)/shard_map/ppermute | solution.py:17
  64.7 22.4 %collective-permute-start.10 = (bf16[256,1024]{1,0:T(8,128)(2,1)S(1)}, bf16[256,1024]{1,0:T(8,128)(2,1)S(1)}, u32[]{:S(2)}, u32[]{:S(2)}) collective-permute-start(bf16[256,1024]{1,0:T(8,128)(2,1)S(1)} %shard_map.62.line_ref.refs_0_), channel_id=1, source_target_pairs={{0,1},{1,0},{2,3},{3,2},{4,5},{5,4},{6,7},{7,6},{8,9},{9,8},{10,11... | collective-permute-start | bytes 1572872 | tf_op jit(solution)/shard_map/ppermute | solution.py:17
  66.7 15.5 %collective-permute-start = (bf16[64,1024]{1,0:T(8,128)(2,1)S(1)}, bf16[64,1024]{1,0:T(8,128)(2,1)S(1)}, u32[]{:S(2)}, u32[]{:S(2)}) collective-permute-start(bf16[64,1024]{1,0:T(8,128)(2,1)S(1)} %get-tuple-element.35), channel_id=1, source_target_pairs={{0,2},{1,3},{2,0},{3,1},{4,6},{5,7},{6,4},{7,5},{8,10},{9,11},{10,... | collective-permute-start | bytes 393224 | tf_op jit(solution)/shard_map/ppermute | solution.py:17
  71.5 13.3 %collective-permute-start.1 = (bf16[64,1024]{1,0:T(8,128)(2,1)S(1)}, bf16[64,1024]{1,0:T(8,128)(2,1)S(1)}, u32[]{:S(2)}, u32[]{:S(2)}) collective-permute-start(bf16[64,1024]{1,0:T(8,128)(2,1)S(1)} %get-tuple-element.36), channel_id=1, source_target_pairs={{0,4},{1,5},{2,6},{3,7},{4,0},{5,1},{6,2},{7,3},{8,12},{9,13},{10,... | collective-permute-start | bytes 393224 | tf_op jit(solution)/shard_map/ppermute | solution.py:17
  77.3 8.5 %collective-permute-start.2 = (bf16[64,1024]{1,0:T(8,128)(2,1)S(1)}, bf16[64,1024]{1,0:T(8,128)(2,1)S(1)}, u32[]{:S(2)}, u32[]{:S(2)}) collective-permute-start(bf16[64,1024]{1,0:T(8,128)(2,1)S(1)} %get-tuple-element.37), channel_id=1, source_target_pairs={{0,6},{1,7},{2,4},{3,5},{4,2},{5,3},{6,0},{7,1},{8,14},{9,15},{10,... | collective-permute-start | bytes 393224 | tf_op jit(solution)/shard_map/ppermute | solution.py:17
  81.3 8.3 %collective-permute-start.17 = (bf16[64,1024]{1,0:T(8,128)(2,1)S(1)}, bf16[64,1024]{1,0:T(8,128)(2,1)S(1)}, u32[]{:S(2)}, u32[]{:S(2)}) collective-permute-start(bf16[64,1024]{1,0:T(8,128)(2,1)S(1)} %get-tuple-element.51), channel_id=1, source_target_pairs={{0,2},{1,3},{2,0},{3,1},{4,6},{5,7},{6,4},{7,5},{8,10},{9,11},{10,... | collective-permute-start | bytes 393224 | tf_op jit(solution)/shard_map/ppermute | solution.py:17
  82.2 11.9 %collective-permute-start.18 = (bf16[64,1024]{1,0:T(8,128)(2,1)S(1)}, bf16[64,1024]{1,0:T(8,128)(2,1)S(1)}, u32[]{:S(2)}, u32[]{:S(2)}) collective-permute-start(bf16[64,1024]{1,0:T(8,128)(2,1)S(1)} %get-tuple-element.52), channel_id=1, source_target_pairs={{0,4},{1,5},{2,6},{3,7},{4,0},{5,1},{6,2},{7,3},{8,12},{9,13},{10,... | collective-permute-start | bytes 393224 | tf_op jit(solution)/shard_map/ppermute | solution.py:17
  84.8 9.3 %collective-permute-start.19 = (bf16[64,1024]{1,0:T(8,128)(2,1)S(1)}, bf16[64,1024]{1,0:T(8,128)(2,1)S(1)}, u32[]{:S(2)}, u32[]{:S(2)}) collective-permute-start(bf16[64,1024]{1,0:T(8,128)(2,1)S(1)} %get-tuple-element.53), channel_id=1, source_target_pairs={{0,6},{1,7},{2,4},{3,5},{4,2},{5,3},{6,0},{7,1},{8,14},{9,15},{10,... | collective-permute-start | bytes 393224 | tf_op jit(solution)/shard_map/ppermute | solution.py:17
  86.5 12.8 %collective-permute-start.3 = (bf16[256,512]{1,0:T(8,128)(2,1)S(1)}, bf16[256,512]{1,0:T(8,128)(2,1)S(1)}, u32[]{:S(2)}, u32[]{:S(2)}) collective-permute-start(bf16[256,512]{1,0:T(8,128)(2,1)S(1)} %get-tuple-element.39), channel_id=1, source_target_pairs={{0,1},{1,0},{2,3},{3,2},{4,5},{5,4},{6,7},{7,6},{8,9},{9,8},{10,11... | collective-permute-start | bytes 786440 | tf_op jit(solution)/shard_map/ppermute | solution.py:17
  94.3 8.3 %collective-permute-start.22 = (bf16[64,1024]{1,0:T(8,128)(2,1)S(1)}, bf16[64,1024]{1,0:T(8,128)(2,1)S(1)}, u32[]{:S(2)}, u32[]{:S(2)}) collective-permute-start(bf16[64,1024]{1,0:T(8,128)(2,1)S(1)} %shard_map.69.refs_0_), channel_id=1, source_target_pairs={{0,6},{1,7},{2,4},{3,5},{4,2},{5,3},{6,0},{7,1},{8,14},{9,15},{10,... | collective-permute-start | bytes 393224 | tf_op jit(solution)/shard_map/ppermute | solution.py:17
  97.2 9.9 %collective-permute-start.20 = (bf16[64,1024]{1,0:T(8,128)(2,1)S(1)}, bf16[64,1024]{1,0:T(8,128)(2,1)S(1)}, u32[]{:S(2)}, u32[]{:S(2)}) collective-permute-start(bf16[64,1024]{1,0:T(8,128)(2,1)S(1)} %shard_map.69.refs_0_), channel_id=1, source_target_pairs={{0,2},{1,3},{2,0},{3,1},{4,6},{5,7},{6,4},{7,5},{8,10},{9,11},{10,... | collective-permute-start | bytes 393224 | tf_op jit(solution)/shard_map/ppermute | solution.py:17
  98.5 14.0 %collective-permute-start.21 = (bf16[64,1024]{1,0:T(8,128)(2,1)S(1)}, bf16[64,1024]{1,0:T(8,128)(2,1)S(1)}, u32[]{:S(2)}, u32[]{:S(2)}) collective-permute-start(bf16[64,1024]{1,0:T(8,128)(2,1)S(1)} %shard_map.69.refs_0_), channel_id=1, source_target_pairs={{0,4},{1,5},{2,6},{3,7},{4,0},{5,1},{6,2},{7,3},{8,12},{9,13},{10,... | collective-permute-start | bytes 393224 | tf_op jit(solution)/shard_map/ppermute | solution.py:17
  98.8 13.7 %collective-permute-start.23 = (bf16[64,1024]{1,0:T(8,128)(2,1)S(1)}, bf16[64,1024]{1,0:T(8,128)(2,1)S(1)}, u32[]{:S(2)}, u32[]{:S(2)}) collective-permute-start(bf16[64,1024]{1,0:T(8,128)(2,1)S(1)} %shard_map.69.refs_0_), channel_id=1, source_target_pairs={{0,1},{1,0},{2,3},{3,2},{4,5},{5,4},{6,7},{7,6},{8,9},{9,8},{10,11... | collective-permute-start | bytes 393224 | tf_op jit(solution)/shard_map/ppermute | solution.py:17
  99.3 13.2 %collective-permute-start.24 = (bf16[64,1024]{1,0:T(8,128)(2,1)S(1)}, bf16[64,1024]{1,0:T(8,128)(2,1)S(1)}, u32[]{:S(2)}, u32[]{:S(2)}) collective-permute-start(bf16[64,1024]{1,0:T(8,128)(2,1)S(1)} %shard_map.69.refs_0_), channel_id=1, source_target_pairs={{0,3},{1,2},{2,1},{3,0},{4,7},{5,6},{6,5},{7,4},{8,11},{9,10},{10,... | collective-permute-start | bytes 393224 | tf_op jit(solution)/shard_map/ppermute | solution.py:17
  102.6 11.5 %collective-permute-start.25 = (bf16[64,1024]{1,0:T(8,128)(2,1)S(1)}, bf16[64,1024]{1,0:T(8,128)(2,1)S(1)}, u32[]{:S(2)}, u32[]{:S(2)}) collective-permute-start(bf16[64,1024]{1,0:T(8,128)(2,1)S(1)} %shard_map.69.refs_0_), channel_id=1, source_target_pairs={{0,5},{1,4},{2,7},{3,6},{4,1},{5,0},{6,3},{7,2},{8,13},{9,12},{10,... | collective-permute-start | bytes 393224 | tf_op jit(solution)/shard_map/ppermute | solution.py:17
  107.0 7.1 %collective-permute-start.26 = (bf16[64,1024]{1,0:T(8,128)(2,1)S(1)}, bf16[64,1024]{1,0:T(8,128)(2,1)S(1)}, u32[]{:S(2)}, u32[]{:S(2)}) collective-permute-start(bf16[64,1024]{1,0:T(8,128)(2,1)S(1)} %collective-permute-done.22.refs_3_), channel_id=1, source_target_pairs={{0,1},{1,0},{2,3},{3,2},{4,5},{5,4},{6,7},{7,6},{8,9},{9,8},{10,11... | collective-permute-start | bytes 393224 | tf_op jit(solution)/shard_map/ppermute | solution.py:17
  115.1 2.0 %collective-permute-start.28 = (f32[128,1024]{1,0:T(8,128)S(1)}, f32[128,1024]{1,0:T(8,128)S(1)}, u32[]{:S(2)}, u32[]{:S(2)}) collective-permute-start(f32[128,1024]{1,0:T(8,128)S(1)} %get-tuple-element.58), channel_id=1, source_target_pairs={{0,8},{8,0},{16,24},{24,16},{1,9},{9,1},{17,25},{25,17},{2,10},{10... | collective-permute-start | bytes 1572872 | tf_op jit(solution)/shard_map/ppermute | solution.py:17
  116.3 2.3 %collective-permute-start.27 = (f32[128,1024]{1,0:T(8,128)S(1)}, f32[128,1024]{1,0:T(8,128)S(1)}, u32[]{:S(2)}, u32[]{:S(2)}) collective-permute-start(f32[128,1024]{1,0:T(8,128)S(1)} %get-tuple-element.56), channel_id=1, source_target_pairs={{0,8},{8,0},{16,24},{24,16},{1,9},{9,1},{17,25},{25,17},{2,10},{10... | collective-permute-start | bytes 1572872 | tf_op jit(solution)/shard_map/ppermute | solution.py:17
  117.1 8.4 %collective-permute-start.29 = (bf16[128,1024]{1,0:T(8,128)(2,1)S(1)}, bf16[128,1024]{1,0:T(8,128)(2,1)S(1)}, u32[]{:S(2)}, u32[]{:S(2)}) collective-permute-start(bf16[128,1024]{1,0:T(8,128)(2,1)S(1)} %shard_map.72), channel_id=1, source_target_pairs={{0,16},{8,24},{16,0},{24,8},{1,17},{9,25},{17,1},{25,9},{2,18},{10... | collective-permute-start | bytes 786440 | tf_op jit(solution)/shard_map/ppermute | solution.py:17

commit v3 on v2

--- a/solution.py
+++ b/solution.py
@@ -7,7 +7,6 @@
 
 kernel_scale = 32.0
 F32, BF16 = jnp.float32, jnp.bfloat16
-SMEM = pl.BlockSpec(memory_space=pltpu.SMEM)
 VMEM = pl.BlockSpec(memory_space=pltpu.VMEM)
 HBM = pl.BlockSpec(memory_space=pltpu.HBM)
 
@@ -17,7 +16,12 @@
     return lax.ppermute(value, axis, [(i, i ^ mask) for i in range(count)])
 
 
-def call(body, scalars, arrays, outs, flops, scratch=(), to_hbm=False, from_hbm=0):
+def here():
+    gen, bank = lax.axis_index("gen"), lax.axis_index("bank")
+    return gen >> 1, gen & 1, bank >> 1, bank & 1
+
+
+def call(body, arrays, outs, flops, scratch=(), to_hbm=False, from_hbm=0):
     far_away = [i >= len(arrays) - from_hbm for i in range(len(arrays))]
     arrays = [
         pltpu.with_memory_space_constraint(a, pltpu.HBM if there else pltpu.VMEM)
@@ -25,26 +29,26 @@
     ]
     make = jax.ShapeDtypeStruct if to_hbm else pltpu.VMEM
     size = sum(a.size * a.dtype.itemsize for a in arrays)
-    head = [] if scalars is None else [scalars]
     return pl.pallas_call(
         body,
-        in_specs=[SMEM] * len(head) + [HBM if there else VMEM for there in far_away],
+        in_specs=[HBM if there else VMEM for there in far_away],
         out_specs=[HBM if to_hbm else VMEM] * len(outs),
         out_shape=[make(dims, dtype) for dims, dtype in outs],
         scratch_shapes=list(scratch),
         compiler_params=pltpu.CompilerParams(vmem_limit_bytes=24 << 20),
         cost_estimate=pl.CostEstimate(flops=flops, bytes_accessed=size, transcendentals=0),
-    )(*head, *arrays)
-
-
-def modulate(place, latents, shift, scale_mod, bank):
+    )(*arrays)
+
+
+def modulate(latents, shift, scale_mod, bank):
     samples, depth = latents.shape
     rows = 16
     quarter = depth // 4
     steps = samples // rows
     forward, direct = shares(bank.shape[0])
 
-    def body(place, *refs):
+    def body(*refs):
+        place = here()
         sources, bank_hbm = refs[:3], refs[3]
         hid_ref, lent_ref, own_ref, f_ref, d_ref = refs[4:9]
         held, sems, row_sems = refs[9:12], refs[12], refs[13]
@@ -84,7 +88,6 @@
     width = bank.shape[1]
     return call(
         body,
-        place,
         [latents, shift, scale_mod, bank],
         [
             ((samples, depth), BF16),
@@ -110,7 +113,7 @@
         ) + jnp.dot(x_ref[:, quarter:], v_ref[...], preferred_element_type=F32)
 
     return call(
-        body, None, [block, first, second], [((samples, width), F32)], 4 * samples * quarter * width
+        body, [block, first, second], [((samples, width), F32)], 4 * samples * quarter * width
     )[0]
 
 
@@ -126,7 +129,6 @@
     samples, width = part.shape
     return call(
         body,
-        None,
         [part, other],
         [((samples, width), F32), ((samples, width), BF16), ((samples, 128), F32)],
         6 * samples * width,
@@ -149,19 +151,19 @@
 
     return call(
         body,
-        None,
         [forward, direct],
         [(forward.shape, BF16), (direct.shape, BF16)],
         8 * (forward.size + direct.size),
     )
 
 
-def stage(place, hidden, weight, n_bank):
+def stage(hidden, weight, n_bank):
     samples, depth = hidden.shape
     pair = depth // 4 // n_bank * 2
     count = n_bank // 2 if pair % 256 == 0 else 0
 
-    def body(place, hid_ref, w_hbm, o_ref, *refs):
+    def body(hid_ref, w_hbm, o_ref, *refs):
+        place = here()
         copy = pltpu.make_async_copy(w_hbm, o_ref, refs[-1])
         copy.start()
         for i, ref in enumerate(refs[:-1]):
@@ -172,7 +174,6 @@
 
     weight, *pieces = call(
         body,
-        place,
         [hidden, weight],
         [(weight.shape, BF16)] + [((samples, 4 * pair), BF16)] * count,
         0,
@@ -200,7 +201,6 @@
 
     return call(
         body,
-        None,
         [bank],
         [(bank.shape, BF16)],
         8 * bank.size,
@@ -217,7 +217,7 @@
         for i in range(count):
             refs[-1][i * samples : (i + 1) * samples] = refs[i][...]
 
-    return call(body, None, pieces, [((count * samples, width), BF16)], 0)[0]
+    return call(body, pieces, [((count * samples, width), BF16)], 0)[0]
 
 
 def bank_sums(line, blocks, before=None, samples=None):
@@ -227,12 +227,11 @@
     def body(*refs):
         line_ref, rest = refs[0], refs[1:]
         row_refs, rest = rest[: len(blocks)], rest[len(blocks) :]
-        outs, sums = rest[-1 - count : -1], rest[-1]
-        started = before is not None
-        if started:
-            sums[...] = rest[0][...]
+        held = None if before is None else rest[0]
+        outs = rest[-count - (count > 1) :][:count]
+        sums = rest[-1]
         for block, ref in zip(blocks, row_refs):
-            tile = min(512, block.shape[0])
+            tile = min(1024, block.shape[0])
             for start in range(0, block.shape[0], tile):
                 rows = ref[start : start + tile]
                 scores = lax.dot_general(
@@ -240,20 +239,19 @@
                 )
                 weight = jnp.exp(kernel_scale * scores).astype(BF16)
                 term = jnp.dot(weight, rows, preferred_element_type=F32)
-                sums[...] = sums[...] + term if started else term
-                started = True
-        for i, ref in enumerate(outs):
-            size = total // count
-            ref[...] = sums[i * size : (i + 1) * size].astype(ref.dtype)
+                sums[...] = term if held is None else held[...] + term
+                held = sums
+        if count > 1:
+            for i, ref in enumerate(outs):
+                ref[...] = sums[i * samples : (i + 1) * samples].astype(ref.dtype)
 
     dims = (total // count, width)
     return call(
         body,
-        None,
         [line] + list(blocks) + ([] if before is None else [before]),
         [(dims, BF16 if i else F32) for i in range(count)],
         4 * total * width * sum(block.shape[0] for block in blocks),
-        [pltpu.VMEM((total, width), F32)],
+        [pltpu.VMEM((total, width), F32)] * (count > 1),
     )
 
 
@@ -279,39 +277,46 @@
         out_ref[...] = total / (batch - 1)
 
     return call(
-        body, None, [unit, line, across], [((samples, width), F32)], 4 * samples * width * batch
+        body, [unit, line, across], [((samples, width), F32)], 4 * samples * width * batch
     )[0]
 
 
 def embed_gradient(near, far, parts, exact, length, bank_rows):
     count = len(parts)
+    samples, width = near.shape
+    half = width // 2
 
     def body(*refs):
+        place = here()
         near_ref, far_ref, exact_ref, length_ref = refs[:4]
+        keep_ref, give_ref = refs[-2:]
         total = far_ref[...]
         for ref in refs[4 : 4 + count]:
             total = total + ref[...].astype(F32)
         proof = near_ref[...] - total / bank_rows
         exact = exact_ref[...]
         radial = jnp.sum(exact * proof, axis=1, keepdims=True)
-        refs[-1][...] = ((proof - exact * radial) / length_ref[:, :1]).astype(BF16)
-
-    samples, width = near.shape
-    return call(
-        body,
-        None,
+        grad = (proof - exact * radial) / length_ref[:, :1]
+        first = place[0] == 0
+        left, right = grad[:, :half], grad[:, half:]
+        keep_ref[...] = jnp.where(first, left, right).astype(BF16)
+        give_ref[...] = jnp.where(first, right, left).astype(BF16)
+
+    return call(
+        body,
         [near, far, exact, length] + list(parts),
-        [((samples, width), BF16)],
+        [((samples, half), BF16)] * 2,
         (count + 8) * samples * width,
-    )[0]
-
-
-def split_pairs(place, pieces):
+    )
+
+
+def split_pairs(pieces):
     samples, width = pieces[0].shape
     block = width // 8
     count = len(pieces)
 
-    def body(place, *refs):
+    def body(*refs):
+        place = here()
         ins, outs = refs[:count], refs[count:]
         for out, y in zip(outs, (place[3], 1 - place[3])):
             for i, ref in enumerate(ins):
@@ -321,7 +326,7 @@
                         :, pl.ds(start, block)
                     ]
 
-    return call(body, place, pieces, [((count * samples, 4 * block), BF16)] * 2, 0)
+    return call(body, pieces, [((count * samples, 4 * block), BF16)] * 2, 0)
 
 
 def turn(kept, given):
@@ -331,79 +336,86 @@
         o_ref[:, :rows] = a_ref[...].T
         o_ref[:, rows:] = b_ref[...].T
 
-    return call(body, None, [kept, given], [((width, 2 * rows), BF16)], 0)[0]
-
-
-def feature_sums(place, columns, grads, blocks):
-    samples, width = grads[0].shape
-    count = len(grads)
-    piece = columns.shape[0] // 4
-    batch = columns.shape[1]
-    fresh = count > 1
-
-    def body(place, cols_ref, *refs):
-        ins, outs = refs[:count], refs[count:]
-        held = outs[-1] if fresh else ins[0]
+    return call(body, [kept, given], [((width, 2 * rows), BF16)], 0)[0]
+
+
+def feature_sums(columns, grads, core):
+    fresh = len(grads) > 1
+    arrays = [array for group in grads for array in group]
+    samples = sum(array.shape[0] for array in grads[0]) // 2
+    width = arrays[0].shape[1]
+    batch = len(grads) * samples
+    piece = columns[0].shape[0] // 4
+
+    def body(own_ref, other_ref, *refs):
+        place = here()
+        outs = refs[len(arrays) :]
+        held = outs[-1] if fresh else refs[0]
         if fresh:
-            for i in range(count):
-                held[i * samples : (i + 1) * samples] = ins[i][...]
-        for ref, (side, core) in zip(outs, blocks):
+            ins = iter(refs)
+            for i, group in enumerate(grads):
+                own = next(ins)
+                if len(group) > 1:
+                    own, other = own[...], next(ins)[...]
+                else:
+                    own, other = own[:samples], own[samples:]
+                held[i * samples : (i + 1) * samples] = own
+                held[batch + i * samples : batch + (i + 1) * samples] = other
+        for side in (0, 1):
             start = 2 * (place[0] ^ side) + (place[1] ^ core)
             start = pl.multiple_of(start * piece, piece)
-            ref[...] = jnp.dot(
-                cols_ref[pl.ds(start, piece), :], held[...], preferred_element_type=F32
+            outs[0][side * piece : (side + 1) * piece] = jnp.dot(
+                own_ref[pl.ds(start, piece), :], held[:batch], preferred_element_type=F32
+            ) + jnp.dot(
+                other_ref[pl.ds(start, piece), :], held[batch:], preferred_element_type=F32
             )
 
     return call(
         body,
-        place,
-        [columns] + list(grads),
-        [((piece, width), F32)] * len(blocks) + [((batch, width), BF16)] * fresh,
-        2 * len(blocks) * piece * width * batch,
-    )
-
-
-def add_round(a, b):
-    def body(a_ref, b_ref, o_ref):
-        o_ref[...] = (a_ref[...] + b_ref[...]).astype(BF16)
-
-    return call(body, None, [a, b], [(a.shape, BF16)], a.size)[0]
-
-
-def square_sums(kept, from_core, from_side, devices):
-    rows, width = kept.shape
-
-    def body(a_ref, b_ref, c_ref, grad_ref, out_ref):
-        grad = a_ref[...] + b_ref[...] + c_ref[...].astype(F32)
-        grad_ref[...] = grad
-        squares = jnp.sum((grad * grad).reshape(rows // 8, 8, width), axis=0)
-        tile = squares[:, :128]
+        list(columns) + arrays,
+        [((2 * piece, width), F32)] + [((2 * batch, width), BF16)] * fresh,
+        8 * piece * width * batch,
+    )
+
+
+def square_sums(kept, taken, devices):
+    rows, width = kept.shape[0] // 2, kept.shape[1]
+
+    def body(a_ref, b_ref, home_ref, away_ref, out_ref):
+        total = 0.0
+        for ref, at in ((home_ref, slice(0, rows)), (away_ref, slice(rows, 2 * rows))):
+            block = a_ref[at] + b_ref[at]
+            ref[...] = block
+            total = total + jnp.sum((block * block).reshape(rows // 8, 8, width), axis=0)
+        tile = total[:, :128]
         for i in range(1, width // 128):
-            tile = tile + squares[:, i * 128 : (i + 1) * 128]
+            tile = tile + total[:, i * 128 : (i + 1) * 128]
         tile = jnp.sum(tile, axis=0, keepdims=True)
         out_ref[...] = jnp.broadcast_to(tile[None], out_ref.shape)
 
     return call(
         body,
-        None,
-        [kept, from_core, from_side],
-        [((rows, width), F32), ((devices, 1, 128), F32)],
-        4 * rows * width,
-    )
-
-
-def scaled(gradient, squares, entries):
-    rows = gradient.shape[0]
+        [kept, taken],
+        [((rows, width), F32)] * 2 + [((devices, 1, 128), F32)],
+        8 * rows * width,
+    )
+
+
+def scaled(home, other, squares, entries):
+    rows, half = home.shape
     steps = 4 if rows % 32 == 0 else 1
     size = rows // steps
 
-    def body(g_ref, s_ref, o_hbm, held, sems):
+    def body(h_ref, a_ref, s_ref, o_hbm, held, sems):
+        place = here()
         mean = jnp.sum(s_ref[...]) / entries
         factor = lax.rsqrt(jnp.full((1, 1), mean + 1e-06, F32))
         copies = []
         for i in range(steps):
             at = slice(i * size, (i + 1) * size)
-            held[at] = g_ref[at] * factor
+            first = place[0] == 0
+            held[at, :half] = jnp.where(first, h_ref[at], a_ref[at]) * factor
+            held[at, half:] = jnp.where(first, a_ref[at], h_ref[at]) * factor
             copies.append(
                 pltpu.make_async_copy(held.at[at], o_hbm.at[pl.ds(i * size, size)], sems.at[i])
             )
@@ -411,24 +423,26 @@
         for copy in copies:
             copy.wait()
 
-    return call(
-        body,
-        None,
-        [gradient, squares],
-        [(gradient.shape, F32)],
-        gradient.size,
-        [pltpu.VMEM(gradient.shape, F32), pltpu.SemaphoreType.DMA((steps,))],
+    dims = (rows, 2 * half)
+    return call(
+        body,
+        [home, other, squares],
+        [(dims, F32)],
+        2 * home.size,
+        [pltpu.VMEM(dims, F32), pltpu.SemaphoreType.DMA((steps,))],
         to_hbm=True,
     )[0]
 
 
-def by_feature(place, hidden, pieces, n_bank):
+def by_feature(hidden, pieces, n_bank):
     samples, depth = hidden.shape
     piece = depth // 4 // n_bank
     if pieces:
         pieces = [swap(p, "bank", 2 * i) if i else p for i, p in enumerate(pieces)]
-        kept, given = split_pairs(place, pieces)
-        return turn(kept, swap(given, "bank", 1))
+        kept, given = split_pairs(pieces)
+        given = swap(given, "bank", 1)
+        return turn(kept, given)
+    place = here()
     pairs = hidden.reshape(samples, 4, n_bank // 2, 2 * piece)
     pieces = [
         lax.dynamic_index_in_dim(pairs, place[2] ^ i, 2, keepdims=False)
@@ -446,22 +460,19 @@
     width = head_weight.shape[1]
     n_gen = lax.axis_size("gen")
     n_bank = lax.axis_size("bank")
-    gen = lax.axis_index("gen")
-    me = lax.axis_index("bank")
-    place = jnp.stack([gen // 2, gen % 2, me // 2, me % 2]).astype(jnp.int32)
     evens, odds = list(range(0, n_bank, 2)), list(range(1, n_bank, 2))
 
     head_other = swap(head_weight, "gen", 1)
-    hidden, lent, own, forward, direct = modulate(place, latents, shift, scale_mod, bank)
+    hidden, lent, own, forward, direct = modulate(latents, shift, scale_mod, bank)
     lent = swap(lent, "gen", 2)
     forward, direct = normalize_sent(forward, direct)
-    head_weight, pieces = stage(place, hidden, head_weight, n_bank)
+    head_weight, pieces = stage(hidden, head_weight, n_bank)
     bank_unit = normalize(bank)
     own_part = project(own, head_weight, head_other)
     returned = swap(project(lent, head_weight, head_other), "gen", 2)
     exact, unit, length = finish_embed(own_part, returned)
 
-    columns = by_feature(place, hidden, pieces, n_bank)
+    columns = by_feature(hidden, pieces, n_bank)
 
     forward = swap(forward, "bank", 1)
     direct = swap(direct, "bank", 1)
@@ -478,21 +489,32 @@
     far = bank_sums(line, late, sums, samples)
     parts = [swap(v, "bank", m) for m, v in zip(evens[1:], far[1:])]
     near = pair_sums(unit, line, across)
-    grad_embed = embed_gradient(near, far[0], parts, exact, length, bank.shape[0] * n_bank)
-
-    grads = {0: grad_embed}
-    for m in range(n_bank - 2, 0, -1):
-        grads[m] = swap(grad_embed, "bank", m)
-    grads[n_bank - 1] = swap(grads[n_bank - 2], "bank", 1)
+    keep, give = embed_gradient(
+        near, far[0], parts, exact, length, bank.shape[0] * n_bank
+    )
+
+    given = swap(give, "gen", 2)
+    both = join([keep, given])
+    high = range(n_bank - 2, n_bank // 2 - 1, -2)
+    grads = {0: [keep, given]}
+    for m in high:
+        grads[m] = [swap(keep, "bank", m)]
+    for m in high:
+        grads[m].append(swap(given, "bank", m))
+    for m in range(n_bank // 2 - 1, 0, -1):
+        grads[m] = [swap(both, "bank", m)]
+    for m in high:
+        ahead = grads[m] if m == high[-1] else [join(grads[m])]
+        grads[m + 1] = [swap(v, "bank", 1) for v in ahead]
     grads = [grads[m] for m in evens + odds]
-    for_core, grads = feature_sums(place, columns, grads, [(1, 1)])
-    for_core = swap(for_core, "gen", 1)
-    away, ours, home = feature_sums(place, columns, [grads], [(1, 0), (0, 0), (0, 1)])
-    away = swap(add_round(away, for_core), "gen", 2)
-    home = swap(home, "gen", 1)
-    gradient, squares = square_sums(ours, home, away, n_gen * n_bank)
+    columns = [columns, swap(columns, "gen", 2)]
+    for_core, grads = feature_sums(columns, grads, 1)
+    taken = swap(for_core, "gen", 1)
+    kept = feature_sums(columns, [[grads]], 0)[0]
+    home, away, squares = square_sums(kept, taken, n_gen * n_bank)
+    away = swap(away, "gen", 2)
     squares = lax.all_to_all(squares, ("gen", "bank"), 0, 0, tiled=True)
-    return scaled(gradient, squares, depth * width)
+    return scaled(home, away, squares, depth * width)
 
 
 def solution(mesh):

time: 138 us -> 127 us (0.920)
  waiting for transfers between devices: 62.4 us -> 42.9 us
  starting transfers between devices: 42.1 us -> 54.5 us
  Pallas kernels: 21.9 us -> 18.7 us
    ppermute x30 -> x34, waiting for transfers between devices: 62.4 us -> 42.9 us  [swap(): return lax.ppermute(value, axis, [(i, i ^ mask) for i in range(count)])]
    ppermute x30 -> x34, starting transfers between devices: 42.1 us -> 54.5 us  [swap(): return lax.ppermute(value, axis, [(i, i ^ mask) for i in range(count)])]
    pallas_call x20 -> x21, Pallas kernels: 21.9 us -> 18.7 us  [call(): pl.pallas_call(body, in_specs=[HBM if there else VMEM for there in far_aw...]
  transfers between devices with their start and end apart: 30 -> 34, of which waited for: 13 -> 15; matrix products, arithmetic and copies ran while one was open for 0% -> 0% of each run, Pallas kernels for 14% -> 14%
where the time goes in v3:
time: 127 us
  starting transfers between devices  54.5 us (43%)
  waiting for transfers between devices  42.9 us (34%)
  Pallas kernels  18.7 us (15%)
  blocking collectives  10.4 us (8%)
    ppermute x34, starting transfers between devices, swap(): return lax.ppermute(value, axis, [(i, i ^ mask) for i in range(count)])  54.5 us
    ppermute x34, waiting for transfers between devices, swap(): return lax.ppermute(value, axis, [(i, i ^ mask) for i in range(count)])  42.9 us
    pallas_call x21, Pallas kernels, call(): pl.pallas_call(body, in_specs=[HBM if there else VMEM for there in far_aw...  18.7 us
    all_to_all x1, blocking collectives, local(): squares = lax.all_to_all(squares, ('gen', 'bank'), 0, 0, tiled=True)  10.4 us
  transfers between devices with their start and end apart: 34, of which 15 were waited for; matrix products, arithmetic and copies ran while one was open for 0% of the time, Pallas kernels for 14%

profile of v3, /device:TPU:0, one launch (start us, length us, event | category | flops | bytes accessed | tf_op | source)
XLA Modules:
  0.0 126.7 jit_solution(10165433905917186504)
XLA Ops:
  0.5 2.0 %shard_map.55 = (bf16[64,4096]{1,0:T(8,128)(2,1)S(1)}, bf16[64,2048]{1,0:T(8,128)(2,1)S(1)}, bf16[64,2048]{1,0:T(8,128)(2,1)S(1)}, bf16[304,1024]{1,0:T(8,128)(2,1)S(1)}, bf16[416,1024]{1,0:T(8,128)(2,1)S(1)}) custom-call(bf16[64,4096]{1,0:T(8,128)(2,1)} %refs_0_.1, bf16[64,4096]{1,0:T(8,128)(2,1)} %refs_1_.1, bf16[64,4096]{1,0:T(8,128)(2,1)} %refs_2_.1, ...), custom_call_target="tpu_custom_call" | custom-call | flops 2097152 | bytes 5767168 | tf_op jit(solution)/shard_map/pallas_call | solution.py:32
  3.1 2.6 %collective-permute-start.12 = (bf16[304,1024]{1,0:T(8,128)(2,1)S(1)}, bf16[304,1024]{1,0:T(8,128)(2,1)S(1)}, u32[]{:S(2)}, u32[]{:S(2)}) collective-permute-start(bf16[304,1024]{1,0:T(8,128)(2,1)S(1)} %get-tuple-element.46), channel_id=1, source_target_pairs={{0,1},{1,0},{2,3},{3,2},{4,5},{5,4},{6,7},{7,6},{8,9},{9,8},{10,11... | collective-permute-start | bytes 1867784 | tf_op jit(solution)/shard_map/ppermute | solution.py:16
  5.8 1.9 %collective-permute-start.6 = (bf16[64,2048]{1,0:T(8,128)(2,1)S(1)}, bf16[64,2048]{1,0:T(8,128)(2,1)S(1)}, u32[]{:S(2)}, u32[]{:S(2)}) collective-permute-start(bf16[64,2048]{1,0:T(8,128)(2,1)S(1)} %get-tuple-element.42), channel_id=1, source_target_pairs={{0,16},{8,24},{16,0},{24,8},{1,17},{9,25},{17,1},{25,9},{2,18},{10... | collective-permute-start | bytes 786440 | tf_op jit(solution)/shard_map/ppermute | solution.py:16
  7.7 12.9 %collective-permute-done.12.refs_2_ = bf16[304,1024]{1,0:T(8,128)(2,1)S(1)} collective-permute-done((bf16[304,1024]{1,0:T(8,128)(2,1)S(1)}, bf16[304,1024]{1,0:T(8,128)(2,1)S(1)}, u32[]{:S(2)}, u32[]{:S(2)}) %collective-permute-start.12) | collective-permute-done | bytes 622624 | tf_op jit(solution)/shard_map/ppermute | solution.py:16
  20.6 2.0 %collective-permute-start.13 = (bf16[304,1024]{1,0:T(8,128)(2,1)S(1)}, bf16[304,1024]{1,0:T(8,128)(2,1)S(1)}, u32[]{:S(2)}, u32[]{:S(2)}) collective-permute-start(bf16[304,1024]{1,0:T(8,128)(2,1)S(1)} %collective-permute-done.12.refs_2_), channel_id=1, source_target_pairs={{0,16},{8,24},{16,0},{24,8},{1,17},{9,25},{17,1},{25,9},{2,18},{10... | collective-permute-start | bytes 1867784 | tf_op jit(solution)/shard_map/ppermute | solution.py:16
  22.6 1.6 %shard_map.56 = (bf16[1024,1024]{1,0:T(8,128)(2,1)S(1)}, bf16[64,1024]{1,0:T(8,128)(2,1)S(1)}, bf16[64,1024]{1,0:T(8,128)(2,1)S(1)}, bf16[64,1024]{1,0:T(8,128)(2,1)S(1)}, bf16[64,1024]{1,0:T(8,128)(2,1)S(1)}) custom-call(bf16[64,4096]{1,0:T(8,128)(2,1)S(1)} %get-tuple-element.33.hid_ref, bf16[1024,1024]{1,0:T(8,128)(2,1)} %w_hbm.1), custom_call_target="tpu_custom_call" | custom-call | bytes 2621440 | tf_op jit(solution)/shard_map/pallas_call | solution.py:32
  25.1 2.1 %collective-permute-start = (bf16[64,1024]{1,0:T(8,128)(2,1)S(1)}, bf16[64,1024]{1,0:T(8,128)(2,1)S(1)}, u32[]{:S(2)}, u32[]{:S(2)}) collective-permute-start(bf16[64,1024]{1,0:T(8,128)(2,1)S(1)} %get-tuple-element.35), channel_id=1, source_target_pairs={{0,2},{1,3},{2,0},{3,1},{4,6},{5,7},{6,4},{7,5},{8,10},{9,11},{10,... | collective-permute-start | bytes 393224 | tf_op jit(solution)/shard_map/ppermute | solution.py:16
  27.2 2.9 %collective-permute-done.refs_1_ = bf16[64,1024]{1,0:T(8,128)(2,1)S(1)} collective-permute-done((bf16[64,1024]{1,0:T(8,128)(2,1)S(1)}, bf16[64,1024]{1,0:T(8,128)(2,1)S(1)}, u32[]{:S(2)}, u32[]{:S(2)}) %collective-permute-start) | collective-permute-done | bytes 131104 | tf_op jit(solution)/shard_map/ppermute | solution.py:16
  30.2 3.0 %collective-permute-start.1 = (bf16[64,1024]{1,0:T(8,128)(2,1)S(1)}, bf16[64,1024]{1,0:T(8,128)(2,1)S(1)}, u32[]{:S(2)}, u32[]{:S(2)}) collective-permute-start(bf16[64,1024]{1,0:T(8,128)(2,1)S(1)} %get-tuple-element.36), channel_id=1, source_target_pairs={{0,4},{1,5},{2,6},{3,7},{4,0},{5,1},{6,2},{7,3},{8,12},{9,13},{10,... | collective-permute-start | bytes 393224 | tf_op jit(solution)/shard_map/ppermute | solution.py:16
  33.2 5.4 %collective-permute-done.15.refs_2_ = bf16[416,1024]{1,0:T(8,128)(2,1)S(1)} collective-permute-done((bf16[416,1024]{1,0:T(8,128)(2,1)S(1)}, bf16[416,1024]{1,0:T(8,128)(2,1)S(1)}, u32[]{:S(2)}, u32[]{:S(2)}) %collective-permute-start.15) | collective-permute-done | bytes 852000 | tf_op jit(solution)/shard_map/ppermute | solution.py:16
  38.6 3.2 %collective-permute-done.7.b_ref = f32[64,1024]{1,0:T(8,128)S(1)} collective-permute-done((f32[64,1024]{1,0:T(8,128)S(1)}, f32[64,1024]{1,0:T(8,128)S(1)}, u32[]{:S(2)}, u32[]{:S(2)}) %collective-permute-start.7) | collective-permute-done | bytes 262176 | tf_op jit(solution)/shard_map/ppermute | solution.py:16
  41.9 3.5 %collective-permute-start.2 = (bf16[64,1024]{1,0:T(8,128)(2,1)S(1)}, bf16[64,1024]{1,0:T(8,128)(2,1)S(1)}, u32[]{:S(2)}, u32[]{:S(2)}) collective-permute-start(bf16[64,1024]{1,0:T(8,128)(2,1)S(1)} %get-tuple-element.37), channel_id=1, source_target_pairs={{0,6},{1,7},{2,4},{3,5},{4,2},{5,3},{6,0},{7,1},{8,14},{9,15},{10,... | collective-permute-start | bytes 393224 | tf_op jit(solution)/shard_map/ppermute | solution.py:16
  46.8 2.1 %collective-permute-done.2.refs_3_ = bf16[64,1024]{1,0:T(8,128)(2,1)S(1)} collective-permute-done((bf16[64,1024]{1,0:T(8,128)(2,1)S(1)}, bf16[64,1024]{1,0:T(8,128)(2,1)S(1)}, u32[]{:S(2)}, u32[]{:S(2)}) %collective-permute-start.2) | collective-permute-done | bytes 131104 | tf_op jit(solution)/shard_map/ppermute | solution.py:16
  48.9 4.3 %collective-permute-start.8 = (bf16[64,1024]{1,0:T(8,128)(2,1)S(1)}, bf16[64,1024]{1,0:T(8,128)(2,1)S(1)}, u32[]{:S(2)}, u32[]{:S(2)}) collective-permute-start(bf16[64,1024]{1,0:T(8,128)(2,1)S(1)} %get-tuple-element.43.refs_0_.unit_ref), channel_id=1, source_target_pairs={{0,2},{1,3},{2,0},{3,1},{4,6},{5,7},{6,4},{7,5},{8,10},{9,11},{10,... | collective-permute-start | bytes 393224 | tf_op jit(solution)/shard_map/ppermute | solution.py:16
  54.6 1.5 %collective-permute-start.3 = (bf16[256,512]{1,0:T(8,128)(2,1)S(1)}, bf16[256,512]{1,0:T(8,128)(2,1)S(1)}, u32[]{:S(2)}, u32[]{:S(2)}) collective-permute-start(bf16[256,512]{1,0:T(8,128)(2,1)S(1)} %get-tuple-element.39), channel_id=1, source_target_pairs={{0,1},{1,0},{2,3},{3,2},{4,5},{5,4},{6,7},{7,6},{8,9},{9,8},{10,11... | collective-permute-start | bytes 786440 | tf_op jit(solution)/shard_map/ppermute | solution.py:16
  56.2 4.9 %collective-permute-start.9 = (bf16[64,1024]{1,0:T(8,128)(2,1)S(1)}, bf16[64,1024]{1,0:T(8,128)(2,1)S(1)}, u32[]{:S(2)}, u32[]{:S(2)}) collective-permute-start(bf16[64,1024]{1,0:T(8,128)(2,1)S(1)} %get-tuple-element.43.refs_0_.unit_ref), channel_id=1, source_target_pairs={{0,4},{1,5},{2,6},{3,7},{4,0},{5,1},{6,2},{7,3},{8,12},{9,13},{10,... | collective-permute-start | bytes 393224 | tf_op jit(solution)/shard_map/ppermute | solution.py:16
  61.0 3.9 %collective-permute-done.9.refs_2_ = bf16[64,1024]{1,0:T(8,128)(2,1)S(1)} collective-permute-done((bf16[64,1024]{1,0:T(8,128)(2,1)S(1)}, bf16[64,1024]{1,0:T(8,128)(2,1)S(1)}, u32[]{:S(2)}, u32[]{:S(2)}) %collective-permute-start.9) | collective-permute-done | bytes 131104 | tf_op jit(solution)/shard_map/ppermute | solution.py:16
  66.1 2.8 %shard_map.65.refs_1_ = bf16[2048,1024]{1,0:T(8,128)(2,1)S(1)} custom-call(bf16[2048,1024]{1,0:T(8,128)(2,1)} %x_hbm.1), custom_call_target="tpu_custom_call" | custom-call | flops 16777216 | bytes 4194304 | tf_op jit(solution)/shard_map/pallas_call | solution.py:32
  69.1 1.6 %collective-permute-start.4 = (bf16[512,512]{1,0:T(8,128)(2,1)S(1)}, bf16[512,512]{1,0:T(8,128)(2,1)S(1)}, u32[]{:S(2)}, u32[]{:S(2)}) collective-permute-start(bf16[512,512]{1,0:T(8,128)(2,1)S(1)} %shard_map.58.own_ref), channel_id=1, source_target_pairs={{0,16},{8,24},{16,0},{24,8},{1,17},{9,25},{17,1},{25,9},{2,18},{10... | collective-permute-start | bytes 1572872 | tf_op jit(solution)/shard_map/ppermute | solution.py:16
  70.7 3.6 %shard_map.66.refs_3_ = f32[256,1024]{1,0:T(8,128)S(1)} custom-call(bf16[256,1024]{1,0:T(8,128)(2,1)S(1)} %shard_map.62.line_ref.refs_0_, bf16[2048,1024]{1,0:T(8,128)(2,1)S(1)} %shard_map.65.refs_1_, bf16[304,1024]{1,0:T(8,128)(2,1)S(1)} %collective-permute-done.12.refs_2_, bf16[304,1024]{1,0:T(8,128)(2,1)S(1)} %collective-permute-done.17.refs_3_), custom_call_target="tpu_custom_call" | custom-call | flops 2785017856 | bytes 5963776 | tf_op jit(solution)/shard_map/pallas_call | solution.py:32
  77.7 3.0 %collective-permute-start.19 = (bf16[64,1024]{1,0:T(8,128)(2,1)S(1)}, bf16[64,1024]{1,0:T(8,128)(2,1)S(1)}, u32[]{:S(2)}, u32[]{:S(2)}) collective-permute-start(bf16[64,1024]{1,0:T(8,128)(2,1)S(1)} %get-tuple-element.52), channel_id=1, source_target_pairs={{0,4},{1,5},{2,6},{3,7},{4,0},{5,1},{6,2},{7,3},{8,12},{9,13},{10,... | collective-permute-start | bytes 393224 | tf_op jit(solution)/shard_map/ppermute | solution.py:16
  83.6 2.4 %collective-permute-done.19.refs_5_ = bf16[64,1024]{1,0:T(8,128)(2,1)S(1)} collective-permute-done((bf16[64,1024]{1,0:T(8,128)(2,1)S(1)}, bf16[64,1024]{1,0:T(8,128)(2,1)S(1)}, u32[]{:S(2)}, u32[]{:S(2)}) %collective-permute-start.19) | collective-permute-done | bytes 131104 | tf_op jit(solution)/shard_map/ppermute | solution.py:16
  86.0 2.3 %collective-permute-done.20.refs_6_ = bf16[64,1024]{1,0:T(8,128)(2,1)S(1)} collective-permute-done((bf16[64,1024]{1,0:T(8,128)(2,1)S(1)}, bf16[64,1024]{1,0:T(8,128)(2,1)S(1)}, u32[]{:S(2)}, u32[]{:S(2)}) %collective-permute-start.20) | collective-permute-done | bytes 131104 | tf_op jit(solution)/shard_map/ppermute | solution.py:16
  89.5 3.1 %collective-permute-start.25 = (bf16[64,512]{1,0:T(8,128)(2,1)S(1)}, bf16[64,512]{1,0:T(8,128)(2,1)S(1)}, u32[]{:S(2)}, u32[]{:S(2)}) collective-permute-start(bf16[64,512]{1,0:T(8,128)(2,1)S(1)} %get-tuple-element.54.refs_0_), channel_id=1, source_target_pairs={{0,6},{1,7},{2,4},{3,5},{4,2},{5,3},{6,0},{7,1},{8,14},{9,15},{10,... | collective-permute-start | bytes 196616 | tf_op jit(solution)/shard_map/ppermute | solution.py:16
  92.6 2.4 %collective-permute-start.23 = (bf16[64,512]{1,0:T(8,128)(2,1)S(1)}, bf16[64,512]{1,0:T(8,128)(2,1)S(1)}, u32[]{:S(2)}, u32[]{:S(2)}) collective-permute-start(bf16[64,512]{1,0:T(8,128)(2,1)S(1)} %get-tuple-element.54.refs_0_), channel_id=1, source_target_pairs={{0,4},{1,5},{2,6},{3,7},{4,0},{5,1},{6,2},{7,3},{8,12},{9,13},{10,... | collective-permute-start | bytes 196616 | tf_op jit(solution)/shard_map/ppermute | solution.py:16
  94.9 2.9 %collective-permute-start.26 = (bf16[64,512]{1,0:T(8,128)(2,1)S(1)}, bf16[64,512]{1,0:T(8,128)(2,1)S(1)}, u32[]{:S(2)}, u32[]{:S(2)}) collective-permute-start(bf16[64,512]{1,0:T(8,128)(2,1)S(1)} %collective-permute-done.21.refs_1_), channel_id=1, source_target_pairs={{0,6},{1,7},{2,4},{3,5},{4,2},{5,3},{6,0},{7,1},{8,14},{9,15},{10,... | collective-permute-start | bytes 196616 | tf_op jit(solution)/shard_map/ppermute | solution.py:16
  99.4 2.1 %collective-permute-start.27 = (bf16[128,512]{1,0:T(8,128)(2,1)S(1)}, bf16[128,512]{1,0:T(8,128)(2,1)S(1)}, u32[]{:S(2)}, u32[]{:S(2)}) collective-permute-start(bf16[128,512]{1,0:T(8,128)(2,1)S(1)} %shard_map.70), channel_id=1, source_target_pairs={{0,1},{1,0},{2,3},{3,2},{4,5},{5,4},{6,7},{7,6},{8,9},{9,8},{10,11... | collective-permute-start | bytes 393224 | tf_op jit(solution)/shard_map/ppermute | solution.py:16
  102.9 1.7 %collective-permute-start.28 = (bf16[128,512]{1,0:T(8,128)(2,1)S(1)}, bf16[128,512]{1,0:T(8,128)(2,1)S(1)}, u32[]{:S(2)}, u32[]{:S(2)}) collective-permute-start(bf16[128,512]{1,0:T(8,128)(2,1)S(1)} %shard_map.70), channel_id=1, source_target_pairs={{0,3},{1,2},{2,1},{3,0},{4,7},{5,6},{6,5},{7,4},{8,11},{9,10},{10,... | collective-permute-start | bytes 393224 | tf_op jit(solution)/shard_map/ppermute | solution.py:16
  107.2 1.7 %collective-permute-done.28.refs_8_ = bf16[128,512]{1,0:T(8,128)(2,1)S(1)} collective-permute-done((bf16[128,512]{1,0:T(8,128)(2,1)S(1)}, bf16[128,512]{1,0:T(8,128)(2,1)S(1)}, u32[]{:S(2)}, u32[]{:S(2)}) %collective-permute-start.28) | collective-permute-done | bytes 131104 | tf_op jit(solution)/shard_map/ppermute | solution.py:16
  108.9 2.0 %collective-permute-done.30.refs_10_ = bf16[64,512]{1,0:T(8,128)(2,1)S(1)} collective-permute-done((bf16[64,512]{1,0:T(8,128)(2,1)S(1)}, bf16[64,512]{1,0:T(8,128)(2,1)S(1)}, u32[]{:S(2)}, u32[]{:S(2)}) %collective-permute-start.30) | collective-permute-done | bytes 65568 | tf_op jit(solution)/shard_map/ppermute | solution.py:16
  113.5 1.9 %collective-permute-start.33 = (f32[128,512]{1,0:T(8,128)S(1)}, f32[128,512]{1,0:T(8,128)S(1)}, u32[]{:S(2)}, u32[]{:S(2)}) collective-permute-start(f32[128,512]{1,0:T(8,128)S(1)} %get-tuple-element.59), channel_id=1, source_target_pairs={{0,16},{8,24},{16,0},{24,8},{1,17},{9,25},{17,1},{25,9},{2,18},{10... | collective-permute-start | bytes 786440 | tf_op jit(solution)/shard_map/ppermute | solution.py:16
  115.4 10.4 %all_to_all.5.s_ref = f32[32,1,128]{2,1,0:T(1,128)S(1)} all-to-all(f32[32,1,128]{2,1,0:T(1,128)S(1)} %get-tuple-element.60), channel_id=1, replica_groups=mesh['gen'=4,'bank'=8] {'gen','bank'}, dimensions={0} | all-to-all | bytes 32768 | tf_op jit(solution)/shard_map/all_to_all | solution.py:516
  (58 shorter events, 22.7 us)
Async XLA Ops:
  0.0 24.2 %collective-permute-start.5 = (bf16[1024,1024]{1,0:T(8,128)(2,1)}, bf16[1024,1024]{1,0:T(8,128)(2,1)S(1)}, u32[]{:S(2)}, u32[]{:S(2)}) collective-permute-start(bf16[1024,1024]{1,0:T(8,128)(2,1)} %w_hbm.1), channel_id=1, source_target_pairs={{0,8},{8,0},{16,24},{24,16},{1,9},{9,1},{17,25},{25,17},{2,10},{10... | collective-permute-start | bytes 6291464 | tf_op jit(solution)/shard_map/ppermute | solution.py:16
  3.1 17.5 %collective-permute-start.12 = (bf16[304,1024]{1,0:T(8,128)(2,1)S(1)}, bf16[304,1024]{1,0:T(8,128)(2,1)S(1)}, u32[]{:S(2)}, u32[]{:S(2)}) collective-permute-start(bf16[304,1024]{1,0:T(8,128)(2,1)S(1)} %get-tuple-element.46), channel_id=1, source_target_pairs={{0,1},{1,0},{2,3},{3,2},{4,5},{5,4},{6,7},{7,6},{8,9},{9,8},{10,11... | collective-permute-start | bytes 1867784 | tf_op jit(solution)/shard_map/ppermute | solution.py:16
  5.7 33.0 %collective-permute-start.15 = (bf16[416,1024]{1,0:T(8,128)(2,1)S(1)}, bf16[416,1024]{1,0:T(8,128)(2,1)S(1)}, u32[]{:S(2)}, u32[]{:S(2)}) collective-permute-start(bf16[416,1024]{1,0:T(8,128)(2,1)S(1)} %get-tuple-element.47), channel_id=1, source_target_pairs={{0,1},{1,0},{2,3},{3,2},{4,5},{5,4},{6,7},{7,6},{8,9},{9,8},{10,11... | collective-permute-start | bytes 2555912 | tf_op jit(solution)/shard_map/ppermute | solution.py:16
  5.8 18.4 %collective-permute-start.6 = (bf16[64,2048]{1,0:T(8,128)(2,1)S(1)}, bf16[64,2048]{1,0:T(8,128)(2,1)S(1)}, u32[]{:S(2)}, u32[]{:S(2)}) collective-permute-start(bf16[64,2048]{1,0:T(8,128)(2,1)S(1)} %get-tuple-element.42), channel_id=1, source_target_pairs={{0,16},{8,24},{16,0},{24,8},{1,17},{9,25},{17,1},{25,9},{2,18},{10... | collective-permute-start | bytes 786440 | tf_op jit(solution)/shard_map/ppermute | solution.py:16
  20.6 26.2 %collective-permute-start.13 = (bf16[304,1024]{1,0:T(8,128)(2,1)S(1)}, bf16[304,1024]{1,0:T(8,128)(2,1)S(1)}, u32[]{:S(2)}, u32[]{:S(2)}) collective-permute-start(bf16[304,1024]{1,0:T(8,128)(2,1)S(1)} %collective-permute-done.12.refs_2_), channel_id=1, source_target_pairs={{0,16},{8,24},{16,0},{24,8},{1,17},{9,25},{17,1},{25,9},{2,18},{10... | collective-permute-start | bytes 1867784 | tf_op jit(solution)/shard_map/ppermute | solution.py:16
  25.0 16.8 %collective-permute-start.7 = (f32[64,1024]{1,0:T(8,128)S(1)}, f32[64,1024]{1,0:T(8,128)S(1)}, u32[]{:S(2)}, u32[]{:S(2)}) collective-permute-start(f32[64,1024]{1,0:T(8,128)S(1)} %shard_map.60), channel_id=1, source_target_pairs={{0,16},{8,24},{16,0},{24,8},{1,17},{9,25},{17,1},{25,9},{2,18},{10... | collective-permute-start | bytes 786440 | tf_op jit(solution)/shard_map/ppermute | solution.py:16
  25.1 5.0 %collective-permute-start = (bf16[64,1024]{1,0:T(8,128)(2,1)S(1)}, bf16[64,1024]{1,0:T(8,128)(2,1)S(1)}, u32[]{:S(2)}, u32[]{:S(2)}) collective-permute-start(bf16[64,1024]{1,0:T(8,128)(2,1)S(1)} %get-tuple-element.35), channel_id=1, source_target_pairs={{0,2},{1,3},{2,0},{3,1},{4,6},{5,7},{6,4},{7,5},{8,10},{9,11},{10,... | collective-permute-start | bytes 393224 | tf_op jit(solution)/shard_map/ppermute | solution.py:16
  27.2 43.5 %collective-permute-start.17 = (bf16[304,1024]{1,0:T(8,128)(2,1)S(1)}, bf16[304,1024]{1,0:T(8,128)(2,1)S(1)}, u32[]{:S(2)}, u32[]{:S(2)}) collective-permute-start(bf16[304,1024]{1,0:T(8,128)(2,1)S(1)} %collective-permute-done.12.refs_2_), channel_id=1, source_target_pairs={{0,8},{8,0},{16,24},{24,16},{1,9},{9,1},{17,25},{25,17},{2,10},{10... | collective-permute-start | bytes 1867784 | tf_op jit(solution)/shard_map/ppermute | solution.py:16
  30.2 16.2 %collective-permute-start.1 = (bf16[64,1024]{1,0:T(8,128)(2,1)S(1)}, bf16[64,1024]{1,0:T(8,128)(2,1)S(1)}, u32[]{:S(2)}, u32[]{:S(2)}) collective-permute-start(bf16[64,1024]{1,0:T(8,128)(2,1)S(1)} %get-tuple-element.36), channel_id=1, source_target_pairs={{0,4},{1,5},{2,6},{3,7},{4,0},{5,1},{6,2},{7,3},{8,12},{9,13},{10,... | collective-permute-start | bytes 393224 | tf_op jit(solution)/shard_map/ppermute | solution.py:16
  38.6 37.2 %collective-permute-start.16 = (bf16[416,1024]{1,0:T(8,128)(2,1)S(1)}, bf16[416,1024]{1,0:T(8,128)(2,1)S(1)}, u32[]{:S(2)}, u32[]{:S(2)}) collective-permute-start(bf16[416,1024]{1,0:T(8,128)(2,1)S(1)} %collective-permute-done.15.refs_2_), channel_id=1, source_target_pairs={{0,8},{8,0},{16,24},{24,16},{1,9},{9,1},{17,25},{25,17},{2,10},{10... | collective-permute-start | bytes 2555912 | tf_op jit(solution)/shard_map/ppermute | solution.py:16
  41.9 7.0 %collective-permute-start.2 = (bf16[64,1024]{1,0:T(8,128)(2,1)S(1)}, bf16[64,1024]{1,0:T(8,128)(2,1)S(1)}, u32[]{:S(2)}, u32[]{:S(2)}) collective-permute-start(bf16[64,1024]{1,0:T(8,128)(2,1)S(1)} %get-tuple-element.37), channel_id=1, source_target_pairs={{0,6},{1,7},{2,4},{3,5},{4,2},{5,3},{6,0},{7,1},{8,14},{9,15},{10,... | collective-permute-start | bytes 393224 | tf_op jit(solution)/shard_map/ppermute | solution.py:16
  46.4 8.2 %collective-permute-start.10 = (bf16[64,1024]{1,0:T(8,128)(2,1)S(1)}, bf16[64,1024]{1,0:T(8,128)(2,1)S(1)}, u32[]{:S(2)}, u32[]{:S(2)}) collective-permute-start(bf16[64,1024]{1,0:T(8,128)(2,1)S(1)} %get-tuple-element.43.refs_0_.unit_ref), channel_id=1, source_target_pairs={{0,6},{1,7},{2,4},{3,5},{4,2},{5,3},{6,0},{7,1},{8,14},{9,15},{10,... | collective-permute-start | bytes 393224 | tf_op jit(solution)/shard_map/ppermute | solution.py:16
  46.8 29.1 %collective-permute-start.14 = (bf16[304,1024]{1,0:T(8,128)(2,1)S(1)}, bf16[304,1024]{1,0:T(8,128)(2,1)S(1)}, u32[]{:S(2)}, u32[]{:S(2)}) collective-permute-start(bf16[304,1024]{1,0:T(8,128)(2,1)S(1)} %collective-permute-done.13.refs_1_), channel_id=1, source_target_pairs={{0,8},{8,0},{16,24},{24,16},{1,9},{9,1},{17,25},{25,17},{2,10},{10... | collective-permute-start | bytes 1867784 | tf_op jit(solution)/shard_map/ppermute | solution.py:16
  48.9 7.3 %collective-permute-start.8 = (bf16[64,1024]{1,0:T(8,128)(2,1)S(1)}, bf16[64,1024]{1,0:T(8,128)(2,1)S(1)}, u32[]{:S(2)}, u32[]{:S(2)}) collective-permute-start(bf16[64,1024]{1,0:T(8,128)(2,1)S(1)} %get-tuple-element.43.refs_0_.unit_ref), channel_id=1, source_target_pairs={{0,2},{1,3},{2,0},{3,1},{4,6},{5,7},{6,4},{7,5},{8,10},{9,11},{10,... | collective-permute-start | bytes 393224 | tf_op jit(solution)/shard_map/ppermute | solution.py:16
  54.6 14.4 %collective-permute-start.3 = (bf16[256,512]{1,0:T(8,128)(2,1)S(1)}, bf16[256,512]{1,0:T(8,128)(2,1)S(1)}, u32[]{:S(2)}, u32[]{:S(2)}) collective-permute-start(bf16[256,512]{1,0:T(8,128)(2,1)S(1)} %get-tuple-element.39), channel_id=1, source_target_pairs={{0,1},{1,0},{2,3},{3,2},{4,5},{5,4},{6,7},{7,6},{8,9},{9,8},{10,11... | collective-permute-start | bytes 786440 | tf_op jit(solution)/shard_map/ppermute | solution.py:16
  56.2 8.7 %collective-permute-start.9 = (bf16[64,1024]{1,0:T(8,128)(2,1)S(1)}, bf16[64,1024]{1,0:T(8,128)(2,1)S(1)}, u32[]{:S(2)}, u32[]{:S(2)}) collective-permute-start(bf16[64,1024]{1,0:T(8,128)(2,1)S(1)} %get-tuple-element.43.refs_0_.unit_ref), channel_id=1, source_target_pairs={{0,4},{1,5},{2,6},{3,7},{4,0},{5,1},{6,2},{7,3},{8,12},{9,13},{10,... | collective-permute-start | bytes 393224 | tf_op jit(solution)/shard_map/ppermute | solution.py:16
  64.9 16.8 %collective-permute-start.11 = (bf16[256,1024]{1,0:T(8,128)(2,1)S(1)}, bf16[256,1024]{1,0:T(8,128)(2,1)S(1)}, u32[]{:S(2)}, u32[]{:S(2)}) collective-permute-start(bf16[256,1024]{1,0:T(8,128)(2,1)S(1)} %shard_map.62.line_ref.refs_0_), channel_id=1, source_target_pairs={{0,1},{1,0},{2,3},{3,2},{4,5},{5,4},{6,7},{7,6},{8,9},{9,8},{10,11... | collective-permute-start | bytes 1572872 | tf_op jit(solution)/shard_map/ppermute | solution.py:16
  69.1 33.8 %collective-permute-start.4 = (bf16[512,512]{1,0:T(8,128)(2,1)S(1)}, bf16[512,512]{1,0:T(8,128)(2,1)S(1)}, u32[]{:S(2)}, u32[]{:S(2)}) collective-permute-start(bf16[512,512]{1,0:T(8,128)(2,1)S(1)} %shard_map.58.own_ref), channel_id=1, source_target_pairs={{0,16},{8,24},{16,0},{24,8},{1,17},{9,25},{17,1},{25,9},{2,18},{10... | collective-permute-start | bytes 1572872 | tf_op jit(solution)/shard_map/ppermute | solution.py:16
  77.3 6.3 %collective-permute-start.18 = (bf16[64,1024]{1,0:T(8,128)(2,1)S(1)}, bf16[64,1024]{1,0:T(8,128)(2,1)S(1)}, u32[]{:S(2)}, u32[]{:S(2)}) collective-permute-start(bf16[64,1024]{1,0:T(8,128)(2,1)S(1)} %get-tuple-element.51), channel_id=1, source_target_pairs={{0,2},{1,3},{2,0},{3,1},{4,6},{5,7},{6,4},{7,5},{8,10},{9,11},{10,... | collective-permute-start | bytes 393224 | tf_op jit(solution)/shard_map/ppermute | solution.py:16
  77.7 8.3 %collective-permute-start.19 = (bf16[64,1024]{1,0:T(8,128)(2,1)S(1)}, bf16[64,1024]{1,0:T(8,128)(2,1)S(1)}, u32[]{:S(2)}, u32[]{:S(2)}) collective-permute-start(bf16[64,1024]{1,0:T(8,128)(2,1)S(1)} %get-tuple-element.52), channel_id=1, source_target_pairs={{0,4},{1,5},{2,6},{3,7},{4,0},{5,1},{6,2},{7,3},{8,12},{9,13},{10,... | collective-permute-start | bytes 393224 | tf_op jit(solution)/shard_map/ppermute | solution.py:16
  80.7 7.6 %collective-permute-start.20 = (bf16[64,1024]{1,0:T(8,128)(2,1)S(1)}, bf16[64,1024]{1,0:T(8,128)(2,1)S(1)}, u32[]{:S(2)}, u32[]{:S(2)}) collective-permute-start(bf16[64,1024]{1,0:T(8,128)(2,1)S(1)} %get-tuple-element.53), channel_id=1, source_target_pairs={{0,6},{1,7},{2,4},{3,5},{4,2},{5,3},{6,0},{7,1},{8,14},{9,15},{10,... | collective-permute-start | bytes 393224 | tf_op jit(solution)/shard_map/ppermute | solution.py:16
  88.5 6.5 %collective-permute-start.21 = (bf16[64,512]{1,0:T(8,128)(2,1)S(1)}, bf16[64,512]{1,0:T(8,128)(2,1)S(1)}, u32[]{:S(2)}, u32[]{:S(2)}) collective-permute-start(bf16[64,512]{1,0:T(8,128)(2,1)S(1)} %get-tuple-element.55), channel_id=1, source_target_pairs={{0,16},{8,24},{16,0},{24,8},{1,17},{9,25},{17,1},{25,9},{2,18},{10... | collective-permute-start | bytes 196616 | tf_op jit(solution)/shard_map/ppermute | solution.py:16
  89.5 9.4 %collective-permute-start.25 = (bf16[64,512]{1,0:T(8,128)(2,1)S(1)}, bf16[64,512]{1,0:T(8,128)(2,1)S(1)}, u32[]{:S(2)}, u32[]{:S(2)}) collective-permute-start(bf16[64,512]{1,0:T(8,128)(2,1)S(1)} %get-tuple-element.54.refs_0_), channel_id=1, source_target_pairs={{0,6},{1,7},{2,4},{3,5},{4,2},{5,3},{6,0},{7,1},{8,14},{9,15},{10,... | collective-permute-start | bytes 196616 | tf_op jit(solution)/shard_map/ppermute | solution.py:16
  92.6 6.8 %collective-permute-start.23 = (bf16[64,512]{1,0:T(8,128)(2,1)S(1)}, bf16[64,512]{1,0:T(8,128)(2,1)S(1)}, u32[]{:S(2)}, u32[]{:S(2)}) collective-permute-start(bf16[64,512]{1,0:T(8,128)(2,1)S(1)} %get-tuple-element.54.refs_0_), channel_id=1, source_target_pairs={{0,4},{1,5},{2,6},{3,7},{4,0},{5,1},{6,2},{7,3},{8,12},{9,13},{10,... | collective-permute-start | bytes 196616 | tf_op jit(solution)/shard_map/ppermute | solution.py:16
  94.9 6.6 %collective-permute-start.26 = (bf16[64,512]{1,0:T(8,128)(2,1)S(1)}, bf16[64,512]{1,0:T(8,128)(2,1)S(1)}, u32[]{:S(2)}, u32[]{:S(2)}) collective-permute-start(bf16[64,512]{1,0:T(8,128)(2,1)S(1)} %collective-permute-done.21.refs_1_), channel_id=1, source_target_pairs={{0,6},{1,7},{2,4},{3,5},{4,2},{5,3},{6,0},{7,1},{8,14},{9,15},{10,... | collective-permute-start | bytes 196616 | tf_op jit(solution)/shard_map/ppermute | solution.py:16
  97.9 6.7 %collective-permute-start.24 = (bf16[64,512]{1,0:T(8,128)(2,1)S(1)}, bf16[64,512]{1,0:T(8,128)(2,1)S(1)}, u32[]{:S(2)}, u32[]{:S(2)}) collective-permute-start(bf16[64,512]{1,0:T(8,128)(2,1)S(1)} %collective-permute-done.21.refs_1_), channel_id=1, source_target_pairs={{0,4},{1,5},{2,6},{3,7},{4,0},{5,1},{6,2},{7,3},{8,12},{9,13},{10,... | collective-permute-start | bytes 196616 | tf_op jit(solution)/shard_map/ppermute | solution.py:16
  98.9 8.3 %collective-permute-start.22 = (bf16[128,512]{1,0:T(8,128)(2,1)S(1)}, bf16[128,512]{1,0:T(8,128)(2,1)S(1)}, u32[]{:S(2)}, u32[]{:S(2)}) collective-permute-start(bf16[128,512]{1,0:T(8,128)(2,1)S(1)} %shard_map.70), channel_id=1, source_target_pairs={{0,2},{1,3},{2,0},{3,1},{4,6},{5,7},{6,4},{7,5},{8,10},{9,11},{10,... | collective-permute-start | bytes 393224 | tf_op jit(solution)/shard_map/ppermute | solution.py:16
  99.4 7.8 %collective-permute-start.27 = (bf16[128,512]{1,0:T(8,128)(2,1)S(1)}, bf16[128,512]{1,0:T(8,128)(2,1)S(1)}, u32[]{:S(2)}, u32[]{:S(2)}) collective-permute-start(bf16[128,512]{1,0:T(8,128)(2,1)S(1)} %shard_map.70), channel_id=1, source_target_pairs={{0,1},{1,0},{2,3},{3,2},{4,5},{5,4},{6,7},{7,6},{8,9},{9,8},{10,11... | collective-permute-start | bytes 393224 | tf_op jit(solution)/shard_map/ppermute | solution.py:16
  102.9 6.0 %collective-permute-start.28 = (bf16[128,512]{1,0:T(8,128)(2,1)S(1)}, bf16[128,512]{1,0:T(8,128)(2,1)S(1)}, u32[]{:S(2)}, u32[]{:S(2)}) collective-permute-start(bf16[128,512]{1,0:T(8,128)(2,1)S(1)} %shard_map.70), channel_id=1, source_target_pairs={{0,3},{1,2},{2,1},{3,0},{4,7},{5,6},{6,5},{7,4},{8,11},{9,10},{10,... | collective-permute-start | bytes 393224 | tf_op jit(solution)/shard_map/ppermute | solution.py:16
  104.6 6.4 %collective-permute-start.31 = (bf16[128,512]{1,0:T(8,128)(2,1)S(1)}, bf16[128,512]{1,0:T(8,128)(2,1)S(1)}, u32[]{:S(2)}, u32[]{:S(2)}) collective-permute-start(bf16[128,512]{1,0:T(8,128)(2,1)S(1)} %shard_map.71), channel_id=1, source_target_pairs={{0,1},{1,0},{2,3},{3,2},{4,5},{5,4},{6,7},{7,6},{8,9},{9,8},{10,11... | collective-permute-start | bytes 393224 | tf_op jit(solution)/shard_map/ppermute | solution.py:16
  105.8 5.1 %collective-permute-start.30 = (bf16[64,512]{1,0:T(8,128)(2,1)S(1)}, bf16[64,512]{1,0:T(8,128)(2,1)S(1)}, u32[]{:S(2)}, u32[]{:S(2)}) collective-permute-start(bf16[64,512]{1,0:T(8,128)(2,1)S(1)} %collective-permute-done.24.refs_4_), channel_id=1, source_target_pairs={{0,1},{1,0},{2,3},{3,2},{4,5},{5,4},{6,7},{7,6},{8,9},{9,8},{10,11... | collective-permute-start | bytes 196616 | tf_op jit(solution)/shard_map/ppermute | solution.py:16
  113.5 12.3 %collective-permute-start.33 = (f32[128,512]{1,0:T(8,128)S(1)}, f32[128,512]{1,0:T(8,128)S(1)}, u32[]{:S(2)}, u32[]{:S(2)}) collective-permute-start(f32[128,512]{1,0:T(8,128)S(1)} %get-tuple-element.59), channel_id=1, source_target_pairs={{0,16},{8,24},{16,0},{24,8},{1,17},{9,25},{17,1},{25,9},{2,18},{10... | collective-permute-start | bytes 786440 | tf_op jit(solution)/shard_map/ppermute | solution.py:16
  (2 other events, 6.2 us)
